TPU v7x, 128 devices: a whole 4x4x4 slice. The times are simulated.
128 devices in a mesh: segment: 4 (over y), blk: 32 (over z, x, core).
Axes of the slice: x: 4, y: 4, z: 4, core: 2. Of those that a mesh axis runs over, the one named last changes fastest.
Arguments:
- echoes: bfloat16 [4, 2048, 128, 512], P('segment', 'blk'), may hold values from -6 to 6
- train_blocks: int32 [4, 256, 6], P('segment', 'blk'), may hold values from 0 to 63, as said below
- hard_bins: int32 [4, 256], P('segment', 'blk'), may hold values 0 or 1
- owner_map: int32 [256], replicated, may hold values from 0 to 255, each once
- code_phase: float32 [64], replicated, may hold values from -3.140625 to 3.140625
Outputs:
- returns: bfloat16 [4, 256, 2048, 256], P('segment', 'blk')
Inputs may be any that keep to these rules, and one draw needn't show every extreme that they name: `train_blocks`: each row lists 6 different training blocks.
All inputs are finite; a program needn't handle non-finite values. No bound on the sum of `hard_bins` on one device may be relied on, other than what follows from the above.
Results may differ from a plain program's by a relative error of at most 0.0086.
Values may be sent and summed in bfloat16 or wider, within the bound.
No kernel may reach another device: no remote copies, remote signals or barrier semaphores. Data moves between devices by JAX's collectives and lax.ppermute only.
A program may use at most 128 MiB of HBM per device.

v0:
```python
import math

import jax
import jax.numpy as jnp
from jax import lax
from jax.experimental import pallas as pl
from jax.experimental.pallas import tpu as pltpu
from jax.sharding import PartitionSpec as P


CH = 128
BEAMS = 128
RB = 32
NTR_EASY = 3
NS_STEPS = 12
CBLK = 128
CHUNKS = (5, 3)
RESIDENT = 3

decay_rate = 0.7
diag_load = 0.1
highest = lax.Precision.HIGHEST
f32 = jnp.float32
bf16 = jnp.bfloat16
MiB = 1 << 20


def params(limit=48):
    return pltpu.CompilerParams(vmem_limit_bytes=limit * MiB)


def shifted(x, by):
    peers = lax.axis_size("segment")
    return lax.ppermute(x, "segment", [(i, (i + by) % peers) for i in range(peers)])


def unit_phasor(index, period):
    eighth = period // 8
    turned = index + eighth
    quadrant = lax.shift_right_logical(turned, int(math.log2(period // 4))) & 3
    rest = (turned & (period // 4 - 1)) - eighth
    x = rest.astype(f32) * (2.0 * math.pi / period)
    x2 = x * x
    sine = x + x * x2 * (-1.0 / 6 + x2 * (1.0 / 120 + x2 * (-1.0 / 5040 + x2 * (1.0 / 362880))))
    cosine = 1.0 + x2 * (
        -0.5 + x2 * (1.0 / 24 + x2 * (-1.0 / 720 + x2 * (1.0 / 40320 - x2 * (1.0 / 3628800))))
    )
    swap = (quadrant & 1) == 1
    c = jnp.where(swap, sine, cosine)
    s = jnp.where(swap, cosine, sine)
    c = jnp.where((quadrant == 1) | (quadrant == 2), -c, c)
    s = jnp.where(quadrant >= 2, -s, s)
    return c, s


def make_doppler_kernel(owners, first, count):
    def doppler_kernel(map_ref, x_hbm, o_hbm, x_ref, table_ref, rows_ref, o_ref, in_sem, out_sem):
        slots = owners * count
        total = map_ref.shape[1]
        bins = total // owners
        pulses = x_ref.shape[2] // 2
        groups, _, rows, _ = o_ref.shape
        pitch = rows_ref.shape[1] // slots
        loads = in_sem.shape[0]
        per_load = x_ref.shape[0] // loads

        def load(i):
            piece = pl.ds(i * per_load, per_load)
            return pltpu.make_async_copy(x_hbm.at[piece], x_ref.at[piece], in_sem.at[i])

        def save(i):
            piece = o_hbm.at[:, pl.ds(i * rows, rows), :]
            return pltpu.make_async_copy(o_ref.at[i], piece, out_sem.at[i])

        for i in range(loads):
            load(i).start()
        slot = lax.broadcasted_iota(jnp.int32, (slots, total), 1)
        row = lax.broadcasted_iota(jnp.int32, (slots, total), 0)
        place = slot % bins - first
        mine = (place >= 0) & (place < count) & (slot // bins * count + place == row)
        chosen = jnp.sum(jnp.where(mine, map_ref[...].astype(f32), 0.0), axis=1, keepdims=True)
        pulse = lax.broadcasted_iota(jnp.int32, (slots, pulses), 1)
        c, s = unit_phasor((pulse * chosen.astype(jnp.int32)) & (pulses - 1), pulses)
        c = (c * (1.0 / math.sqrt(pulses))).astype(bf16)
        s = (s * (1.0 / math.sqrt(pulses))).astype(bf16)
        table_ref[:slots, :pulses] = c
        table_ref[:slots, pulses:] = s
        table_ref[slots:, :pulses] = -s
        table_ref[slots:, pulses:] = c

        def group(i, carry):
            for j in range(loads // groups):
                load(i * (loads // groups) + j).wait()
            for pair in range(rows // 2):
                x = x_ref[pl.ds(i * rows + 2 * pair, 2)].reshape(2 * CH, 2 * pulses)
                d = lax.dot_general(
                    table_ref[...], x, (((1,), (1,)), ((), ())), preferred_element_type=f32
                )
                for part in range(2):
                    for half in range(2):
                        rows_ref[part, pl.ds(2 * pair + half, slots, stride=pitch), :] = d[
                            part * slots : (part + 1) * slots, half * CH : (half + 1) * CH
                        ]
            for part in range(2):
                o_ref[i, :, :, part * CH : (part + 1) * CH] = (
                    rows_ref[part].reshape(slots, pitch, CH)[:, :rows].astype(bf16)
                )
            save(i).start()
            return carry

        lax.fori_loop(0, groups, group, 0)
        for i in range(groups):
            save(i).wait()

    return doppler_kernel


def doppler(samples, owner_map, owners, first, count):
    range_local, channels, double_pulses = samples.shape
    slots = owners * count
    rows, pitch, loads = 16, 24, 8
    groups = range_local // rows
    return pl.pallas_call(
        make_doppler_kernel(owners, first, count),
        out_shape=pltpu.HBM((slots, range_local, 2 * channels), bf16),
        in_specs=[
            pl.BlockSpec(memory_space=pltpu.VMEM),
            pl.BlockSpec(memory_space=pl.ANY),
        ],
        out_specs=pl.BlockSpec(memory_space=pl.ANY),
        scratch_shapes=[
            pltpu.VMEM(samples.shape, bf16),
            pltpu.VMEM((2 * slots, double_pulses), bf16),
            pltpu.VMEM((2, slots * pitch, channels), f32),
            pltpu.VMEM((groups, slots, rows, 2 * channels), bf16),
            pltpu.SemaphoreType.DMA((loads,)),
            pltpu.SemaphoreType.DMA((groups,)),
        ],
        compiler_params=pltpu.CompilerParams(vmem_limit_bytes=67_043_328),
        name="doppler",
    )(owner_map.reshape(1, -1), samples)


def entries(refs):
    return [(ref, j) for ref in refs for j in range(ref.shape[0])]


def make_cov_kernel(first, count, listed):
    def cov_kernel(blocks_ref, hard_ref, y_ref, *refs):
        *o_refs, buf, sem = refs
        per_source = y_ref.shape[2] // RB

        def copy(i, t):
            block = blocks_ref[first + i, t]
            source = block // per_source
            row = pl.multiple_of((block % per_source) * RB, RB)
            return pltpu.make_async_copy(
                y_ref.at[source, i, pl.ds(row, RB), :], buf.at[i, t], sem.at[i, t]
            )

        for i in range(count):
            for t in range(listed):
                copy(i, t).start()
        row_of = lax.broadcasted_iota(jnp.int32, (listed * RB, 1), 0)
        f = lax.broadcasted_iota(jnp.int32, (CH, CH), 0)
        g = lax.broadcasted_iota(jnp.int32, (CH, CH), 1)
        for i in range(count):
            for t in range(listed):
                copy(i, t).wait()
        used = [
            jnp.where(hard_ref[first + i] == 1, listed * RB, NTR_EASY * RB) for i in range(count)
        ]
        rows = [
            buf[i].reshape(listed * RB, 2 * CH) * (row_of < used[i]).astype(f32).astype(bf16)
            for i in range(count)
        ]
        grams = [
            lax.dot_general(y, y, (((0,), (0,)), ((), ())), preferred_element_type=f32)
            for y in rows
        ]
        for i, (o_ref, j) in enumerate(entries(o_refs)):
            re = grams[i][:CH, :CH] + grams[i][CH:, CH:]
            im = grams[i][CH:, :CH] - grams[i][:CH, CH:]
            o_ref[j] = jnp.where(f <= g, re, im) / used[i].astype(f32)

    return cov_kernel


def covariance(owned, blocks, hard, first, pieces):
    count = owned.shape[1]
    listed = blocks.shape[1]
    smem = pl.BlockSpec(memory_space=pltpu.SMEM)
    return pl.pallas_call(
        make_cov_kernel(first, count, listed),
        out_shape=[jax.ShapeDtypeStruct((n, CH, CH), f32) for n in pieces],
        in_specs=[smem, smem, pl.BlockSpec(memory_space=pltpu.HBM)],
        out_specs=[pl.BlockSpec(memory_space=pltpu.VMEM)] * len(pieces),
        scratch_shapes=[
            pltpu.VMEM((count, listed, RB, 2 * CH), bf16),
            pltpu.SemaphoreType.DMA((count, listed)),
        ],
        compiler_params=params(16),
        name="covariance",
    )(blocks, hard, owned)


def halves(z):
    high = z.astype(bf16)
    return high, (z - high.astype(f32)).astype(bf16)


def left(z):
    high, low = halves(z)
    return jnp.concatenate([high, low, high], axis=1)


def right(z):
    high, low = halves(z)

    def real_form(x):
        return jnp.concatenate([x, jnp.concatenate([-x[:, CH:], x[:, :CH]], axis=1)], axis=0)

    big = real_form(high)
    return jnp.concatenate([big, big, real_form(low)], axis=0)


def product(a, b):
    return jnp.dot(a, b, preferred_element_type=f32)


def weights_kernel(*refs):
    *c_refs, o_ref = refs
    parts = len(c_refs) // 3
    earlier_refs = [entries(c_refs[n * parts : (n + 1) * parts]) for n in range(3)]
    count = o_ref.shape[0]
    bins = range(count)
    f = lax.broadcasted_iota(jnp.int32, (CH, CH), 0)
    g = lax.broadcasted_iota(jnp.int32, (CH, CH), 1)
    eye = (f == g).astype(f32)
    eye2 = jnp.concatenate([eye, jnp.zeros_like(eye)], axis=1)
    segment = lax.axis_index("segment")
    decay = [jnp.where(segment > n, decay_rate**n, 0.0) for n in range(3)]
    a, x, e = [], [], []
    for i in bins:
        terms = [decay[n] * ref[j] for n in range(3) for ref, j in (earlier_refs[n][i],)]
        packed = terms[0] + terms[1] + terms[2]
        flipped = packed.T
        re = jnp.where(f <= g, packed, flipped) + diag_load * eye
        im = jnp.where(f > g, packed, jnp.where(f < g, -flipped, 0.0))
        scale = 1.0 / jnp.sum(jnp.sum(re * eye, axis=1, keepdims=True), axis=0, keepdims=True)
        loaded = jnp.concatenate([re, im], axis=1)
        a.append(right(loaded))
        e.append(eye2 - loaded * scale)
        x.append((eye2 + e[i]) * scale)

    def both(x, e):
        return left(jnp.concatenate([x, e], axis=0))

    for turn in range(NS_STEPS // 3):
        if turn == 0:
            e = [product(left(e[i]), right(e[i])) for i in bins]
        else:
            e = [eye2 - product(left(x[i]), a[i]) for i in bins]
        for _ in range(1 if turn == 0 else 2):
            m = [product(both(x[i], e[i]), right(e[i])) for i in bins]
            x = [x[i] + m[i][:CH] for i in bins]
            e = [m[i][CH:] for i in bins]
        x = [x[i] + product(left(x[i]), right(e[i])) for i in bins]

    c, s = unit_phasor((f * (2 * g - BEAMS)) & (2 * BEAMS - 1), 2 * BEAMS)
    steer = jnp.concatenate([c, s], axis=1) * (1.0 / math.sqrt(CH))
    table = right(steer)
    vec = [product(left(x[i]), table) for i in bins]
    for i in bins:
        inner = steer * vec[i]
        gain = jnp.sum(inner[:, :BEAMS] + inner[:, BEAMS:], axis=0, keepdims=True)
        re = (vec[i][:, :BEAMS] / gain).astype(bf16)
        im = (vec[i][:, BEAMS:] / gain).astype(bf16)
        o_ref[i, :CH, :BEAMS] = re
        o_ref[i, :CH, BEAMS:] = -im
        o_ref[i, CH:, :BEAMS] = im
        o_ref[i, CH:, BEAMS:] = re


def beam_weights(parts):
    count = sum(part.shape[0] for part in parts[0])
    vmem = pl.BlockSpec(memory_space=pltpu.VMEM)
    operands = [part for back in parts for part in back]
    return pl.pallas_call(
        weights_kernel,
        out_shape=jax.ShapeDtypeStruct((count, 2 * CH, 2 * BEAMS), bf16),
        in_specs=[vmem] * len(operands),
        out_specs=vmem,
        compiler_params=params(32),
        name="weights",
    )(*operands)


def earlier(cov):
    if len(cov) == 1:
        c3, c1, c2 = (shifted(cov[0], by) for by in (3, 1, 2))
        return [c1], [c2], [c3]
    low, high = cov
    low1, high3 = shifted(low, 1), shifted(high, 3)
    high1, low3 = shifted(high, 1), shifted(low, 3)
    low2, high2 = shifted(low1, 1), shifted(high3, 3)
    return [low1, high1], [low2, high2], [low3, high3]


def compression_table(code_phase, block_len):
    length = code_phase.shape[0]
    input_pos = jnp.arange(2 * block_len, dtype=jnp.int32)[None, :]
    output_pos = jnp.arange(block_len, dtype=jnp.int32)[:, None]
    lag_index = input_pos - output_pos
    onehot = (lag_index[:, :, None] == jnp.arange(length, dtype=jnp.int32)[None, None, :]).astype(
        jnp.float32
    )
    code_table = jnp.stack([jnp.cos(code_phase), jnp.sin(code_phase)]) / math.sqrt(length)
    table = jnp.einsum("pql,kl->kpq", onehot, code_table, precision=highest)
    return table.astype(bf16).reshape(2 * block_len, 2 * block_len)


def compress_kernel(table_ref, y_hbm, z_out, y_ref, in_sem, *held):
    count, sources, per, _ = y_ref.shape
    z_ref, out_sem = held if held else (z_out, None)
    step = CBLK // per
    half = CH

    def load(i):
        return pltpu.make_async_copy(y_hbm.at[:, i], y_ref.at[i], in_sem.at[i])

    def save(i):
        return pltpu.make_async_copy(z_ref.at[i], z_out.at[i], out_sem.at[i])

    for i in range(count):
        load(i).start()
    for i in range(count):
        load(i).wait()
        for start in range(0, sources, step):
            stop = min(start + 2 * step, sources)
            y = y_ref[i, start:stop].reshape((stop - start) * per, 2 * half)
            m = jnp.dot(table_ref[:, : y.shape[0]], y, preferred_element_type=f32)
            r = pl.ds(start * per, CBLK)
            z_ref[i, r, :half] = (m[:CBLK, :half] + m[CBLK:, half:]).astype(bf16)
            z_ref[i, r, half:] = (m[:CBLK, half:] - m[CBLK:, :half]).astype(bf16)
        if held:
            save(i).start()
    if held:
        for i in range(count):
            save(i).wait()


def compress(owned, table):
    sources, count, per, width = owned.shape
    vmem = pl.BlockSpec(memory_space=pltpu.VMEM)
    anywhere = pl.BlockSpec(memory_space=pl.ANY)
    shape = (count, sources * per, width)
    scratch = [
        pltpu.VMEM((count, sources, per, width), bf16),
        pltpu.SemaphoreType.DMA((count,)),
    ]
    if count > RESIDENT:
        scratch += [pltpu.VMEM(shape, bf16), pltpu.SemaphoreType.DMA((count,))]
    return pl.pallas_call(
        compress_kernel,
        out_shape=pltpu.HBM(shape, bf16) if count > RESIDENT else jax.ShapeDtypeStruct(shape, bf16),
        in_specs=[vmem, anywhere],
        out_specs=anywhere if count > RESIDENT else vmem,
        scratch_shapes=scratch,
        compiler_params=params(32),
        name="compress",
    )(table, owned)


def make_beams_kernel(first, aliased):
    def beams_kernel(w_ref, z_in, *refs):
        o_hbm, o_ref, out_sem, *held = refs[aliased:]
        z_ref, in_sem = held if held else (z_in, None)
        count, rows, _ = z_ref.shape
        pieces = out_sem.shape[1]
        step = rows // pieces

        def load(i):
            return pltpu.make_async_copy(z_in.at[i], z_ref.at[i], in_sem.at[i])

        def save(i, p):
            piece = pl.ds(p * step, step)
            return pltpu.make_async_copy(
                o_ref.at[i, piece], o_hbm.at[first + i, piece], out_sem.at[i, p]
            )

        if held:
            for i in range(count):
                load(i).start()
        for i in range(count):
            if held:
                load(i).wait()
            for p in range(pieces):
                r = pl.ds(p * step, step)
                o_ref[i, r] = jnp.dot(
                    z_ref[i, r], w_ref[i], preferred_element_type=f32
                ).astype(bf16)
                save(i, p).start()
        for i in range(count):
            for p in range(pieces):
                save(i, p).wait()

    return beams_kernel


def form_beams(z, weights, held, bins, first):
    count, rows, _ = z.shape
    width = weights.shape[2]
    resident = count <= RESIDENT
    vmem = pl.BlockSpec(memory_space=pltpu.VMEM)
    anywhere = pl.BlockSpec(memory_space=pl.ANY)
    in_specs = [vmem, vmem if resident else anywhere]
    operands = [weights, z]
    aliases = {}
    if held is not None:
        in_specs.append(anywhere)
        operands.append(held)
        aliases = {2: 0}
    pieces = 2 if resident else 1
    scratch = [
        pltpu.VMEM((count, rows, width), bf16),
        pltpu.SemaphoreType.DMA((count, pieces)),
    ]
    if not resident:
        scratch += [pltpu.VMEM(z.shape, bf16), pltpu.SemaphoreType.DMA((count,))]
    return pl.pallas_call(
        make_beams_kernel(first, len(aliases)),
        out_shape=jax.ShapeDtypeStruct((bins, rows, width), bf16),
        in_specs=in_specs,
        out_specs=anywhere,
        scratch_shapes=scratch,
        input_output_aliases=aliases,
        compiler_params=params(32 if resident else 59),
        name="beams",
    )(*operands)


def chain(echoes, train_blocks, hard_bins, owner_map, code_phase):
    samples = echoes[0]
    blocks, hard = train_blocks[0], hard_bins[0]
    owners = lax.axis_size("blk")
    bins = hard.shape[0]
    firsts = [sum(CHUNKS[:i]) for i in range(len(CHUNKS))]
    spectra = []
    for first, count in zip(firsts, CHUNKS):
        sent = doppler(samples, owner_map, owners, first, count)
        spectra.append(sent.reshape(owners, count, samples.shape[0], 2 * CH))
    code_phase, spectra[0] = lax.optimization_barrier((code_phase, spectra[0]))
    table = compression_table(code_phase, CBLK)
    owned = []
    for g, sent in enumerate(spectra):
        if g > 0:
            sent, owned[-1] = lax.optimization_barrier((sent, owned[-1]))
        owned.append(lax.all_to_all(sent, "blk", split_axis=0, concat_axis=0, tiled=True))
    result = None
    for first, y in zip(firsts, owned):
        count = y.shape[1]
        pieces = [count // 2, count - count // 2] if count > 2 else [count]
        parts = earlier(covariance(y, blocks, hard, first, pieces))
        z = compress(y, table)
        weights = beam_weights(parts)
        result = form_beams(z, weights, result, bins, first)
    return result[None]


def solution(mesh):
    in_specs = (
        P("segment", "blk", None, None),
        P("segment", "blk", None),
        P("segment", "blk"),
        P(),
        P(),
    )
    out_specs = P("segment", "blk", None, None)
    return jax.shard_map(chain, mesh=mesh, in_specs=in_specs, out_specs=out_specs, check_vma=False)
```

profile of v0, /device:TPU:0, one launch (start us, length us, event | category | flops | bytes accessed | tf_op | source)
XLA Modules:
  0.0 176.3 jit_solution(13970044497218489111)
XLA Ops:
  0.0 7.8 %doppler.3 = bf16[160,64,256]{2,1,0:T(8,128)(2,1)} custom-call(s32[1,256]{1,0:T(1,128)} %bitcast.25, bf16[64,128,512]{2,1,0:T(8,128)(2,1)} %bitcast.21), custom_call_target="tpu_custom_call" | custom-call | tf_op jit(solution)/shard_map/doppler/pallas_call | solution.py:123
  7.8 8.4 %all-to-all-start = ((bf16[32,5,64,256]{3,2,1,0:T(8,128)(2,1)}), bf16[32,5,64,256]{3,2,1,0:T(8,128)(2,1)}, u32[]{:S(2)}, u32[]{:S(2)}) async-start(bf16[32,5,64,256]{3,2,1,0:T(8,128)(2,1)} %bitcast.23), calls=%async_computation | async-start | bytes 10485760 | tf_op jit(solution)/shard_map/all_to_all | solution.py:459
  16.2 7.1 %doppler.2 = bf16[96,64,256]{2,1,0:T(8,128)(2,1)} custom-call(s32[1,256]{1,0:T(1,128)} %bitcast.26, bf16[64,128,512]{2,1,0:T(8,128)(2,1)} %bitcast.22), custom_call_target="tpu_custom_call" | custom-call | tf_op jit(solution)/shard_map/doppler/pallas_call | solution.py:123
  23.3 0.0 copy-start.2
  23.3 0.0 copy-start.1
  23.3 58.8 %all-to-all-done.y_ref.y_hbm = bf16[32,5,64,256]{3,2,1,0:T(8,128)(2,1)} async-done(((bf16[32,5,64,256]{3,2,1,0:T(8,128)(2,1)}), bf16[32,5,64,256]{3,2,1,0:T(8,128)(2,1)}, u32[]{:S(2)}, u32[]{:S(2)}) %all-to-all-start) | async-done | bytes 5242912 | tf_op jit(solution)/shard_map/all_to_all | solution.py:459
  82.1 4.1 %all-to-all-start.1 = ((bf16[32,3,64,256]{3,2,1,0:T(8,128)(2,1)}), bf16[32,3,64,256]{3,2,1,0:T(8,128)(2,1)S(1)}, u32[]{:S(2)}, u32[]{:S(2)}) async-start(bf16[32,3,64,256]{3,2,1,0:T(8,128)(2,1)} %bitcast.24), calls=%async_computation.1 | async-start | bytes 6291456 | tf_op jit(solution)/shard_map/all_to_all | solution.py:459
  86.2 0.1 copy.7
  86.3 3.0 %covariance.3 = (f32[2,128,128]{2,1,0:T(8,128)}, f32[3,128,128]{2,1,0:T(8,128)}) custom-call(s32[8,6]{1,0:T(8,128)S(1)} %bitcast.17, s32[8]{0:T(128)S(1)} %bitcast.19, bf16[32,5,64,256]{3,2,1,0:T(8,128)(2,1)} %all-to-all-done.y_ref.y_hbm), custom_call_target="tpu_custom_call" | custom-call | tf_op jit(solution)/shard_map/covariance/pallas_call | solution.py:193
  89.3 1.6 collective-permute-start.6
  90.9 1.7 collective-permute-start.11
  92.6 1.8 %collective-permute-start.9 = (f32[3,128,128]{2,1,0:T(8,128)}, f32[3,128,128]{2,1,0:T(8,128)S(1)}, u32[]{:S(2)}, u32[]{:S(2)}) collective-permute-start(f32[3,128,128]{2,1,0:T(8,128)} %get-tuple-element.20), channel_id=1, source_target_pairs={{0,96},{32,0},{64,32},{96,64},{1,97},{33,1},{65,33},{97,65},{2,98}... | collective-permute-start | bytes 589832 | tf_op jit(solution)/shard_map/ppermute | solution.py:34
  94.4 0.2 collective-permute-start.7
  94.6 1.9 %collective-permute-done.6.refs_0_ = f32[2,128,128]{2,1,0:T(8,128)} collective-permute-done((f32[2,128,128]{2,1,0:T(8,128)}, f32[2,128,128]{2,1,0:T(8,128)}, u32[]{:S(2)}, u32[]{:S(2)}) %collective-permute-start.6) | collective-permute-done | bytes 131104 | tf_op jit(solution)/shard_map/ppermute | solution.py:34
  96.5 0.3 collective-permute-start.8
  96.8 31.4 %all-to-all-done.1.y_ref.y_hbm = bf16[32,3,64,256]{3,2,1,0:T(8,128)(2,1)S(1)} async-done(((bf16[32,3,64,256]{3,2,1,0:T(8,128)(2,1)}), bf16[32,3,64,256]{3,2,1,0:T(8,128)(2,1)S(1)}, u32[]{:S(2)}, u32[]{:S(2)}) %all-to-all-start.1) | async-done | bytes 3145760 | tf_op jit(solution)/shard_map/all_to_all | solution.py:459
  128.2 1.7 covariance.2
  129.9 3.1 %collective-permute-start.3 = (f32[2,128,128]{2,1,0:T(8,128)S(1)}, f32[2,128,128]{2,1,0:T(8,128)S(1)}, u32[]{:S(2)}, u32[]{:S(2)}) collective-permute-start(f32[2,128,128]{2,1,0:T(8,128)S(1)} %get-tuple-element.16), channel_id=1, source_target_pairs={{0,96},{32,0},{64,32},{96,64},{1,97},{33,1},{65,33},{97,65},{2,98}... | collective-permute-start | bytes 393224 | tf_op jit(solution)/shard_map/ppermute | solution.py:34
  133.0 0.1 collective-permute-start
  133.1 3.3 %collective-permute-start.10 = (f32[3,128,128]{2,1,0:T(8,128)S(1)}, f32[3,128,128]{2,1,0:T(8,128)S(1)}, u32[]{:S(2)}, u32[]{:S(2)}) collective-permute-start(f32[3,128,128]{2,1,0:T(8,128)S(1)} %collective-permute-done.9.refs_5_), channel_id=1, source_target_pairs={{0,96},{32,0},{64,32},{96,64},{1,97},{33,1},{65,33},{97,65},{2,98}... | collective-permute-start | bytes 589832 | tf_op jit(solution)/shard_map/ppermute | solution.py:34
  136.4 0.1 collective-permute-start.5
  136.5 1.9 %collective-permute-start.1 = (f32[2,128,128]{2,1,0:T(8,128)S(1)}, f32[2,128,128]{2,1,0:T(8,128)S(1)}, u32[]{:S(2)}, u32[]{:S(2)}) collective-permute-start(f32[2,128,128]{2,1,0:T(8,128)S(1)} %get-tuple-element.16), channel_id=1, source_target_pairs={{0,32},{32,64},{64,96},{96,0},{1,33},{33,65},{65,97},{97,1},{2,34}... | collective-permute-start | bytes 393224 | tf_op jit(solution)/shard_map/ppermute | solution.py:34
  138.5 0.8 collective-permute-done.refs_0_
  139.3 3.2 %collective-permute-start.4 = (f32[2,128,128]{2,1,0:T(8,128)S(1)}, f32[2,128,128]{2,1,0:T(8,128)S(1)}, u32[]{:S(2)}, u32[]{:S(2)}) collective-permute-start(f32[2,128,128]{2,1,0:T(8,128)S(1)} %collective-permute-done.3.refs_5_), channel_id=1, source_target_pairs={{0,96},{32,0},{64,32},{96,64},{1,97},{33,1},{65,33},{97,65},{2,98}... | collective-permute-start | bytes 393224 | tf_op jit(solution)/shard_map/ppermute | solution.py:34
  142.5 2.6 %fusion.2 = bf16[2,128,256]{2,0,1:T(2,128)(2,1)S(1)} fusion(s32[128,256]{1,0:T(8,128)S(1)} %iota_subtract_fusion, f32[1,64]{1,0:T(1,128)S(1)} %get-tuple-element.22, f32[1,64]{1,0:T(1,128)S(1)} %get-tuple-element.21), kind=kOutput, calls=%fused_computation.3 | convolution fusion | flops 52494592 | bytes 262656 | tf_op jit(solution)/shard_map/pql,kl->kpq/dot_general | solution.py:319
  145.2 5.9 %compress.3.z_in = bf16[5,2048,256]{2,1,0:T(8,128)(2,1)} custom-call(bf16[256,256]{1,0:T(8,128)(2,1)S(1)} %bitcast.15, bf16[32,5,64,256]{3,2,1,0:T(8,128)(2,1)} %all-to-all-done.y_ref.y_hbm), custom_call_target="tpu_custom_call" | custom-call | tf_op jit(solution)/shard_map/compress/pallas_call | solution.py:364
  151.1 8.1 %weights.3.w_ref = bf16[5,256,256]{2,1,0:T(8,128)(2,1)S(1)} custom-call(f32[2,128,128]{2,1,0:T(8,128)} %collective-permute-done.6.refs_0_, f32[3,128,128]{2,1,0:T(8,128)S(1)} %collective-permute-done.7.refs_1_, f32[2,128,128]{2,1,0:T(8,128)} %collective-permute-done.8.refs_2_, f32[3,128,128]{2,1,0:T(8,128)S(1)} %collective-permute-done.10.refs_3_, ...), custom_call_target="tpu_custom_call" | custom-call | tf_op jit(solution)/shard_map/weights/pallas_call | solution.py:289
  159.2 0.9 copy-done
  160.0 6.6 %beams.2.refs_0_ = bf16[8,2048,256]{2,1,0:T(8,128)(2,1)} custom-call(bf16[5,256,256]{2,1,0:T(8,128)(2,1)} %copy-done, bf16[5,2048,256]{2,1,0:T(8,128)(2,1)} %compress.3.z_in), custom_call_target="tpu_custom_call" | custom-call | tf_op jit(solution)/shard_map/beams/pallas_call | solution.py:431
  166.6 2.4 %compress.2.z_in = bf16[3,2048,256]{2,1,0:T(8,128)(2,1)S(1)} custom-call(bf16[256,256]{1,0:T(8,128)(2,1)S(1)} %bitcast.16, bf16[32,3,64,256]{3,2,1,0:T(8,128)(2,1)S(1)} %all-to-all-done.1.y_ref.y_hbm), custom_call_target="tpu_custom_call" | custom-call | tf_op jit(solution)/shard_map/compress/pallas_call | solution.py:364
  169.0 4.9 %weights.2.w_ref = bf16[3,256,256]{2,1,0:T(8,128)(2,1)S(1)} custom-call(f32[1,128,128]{2,1,0:T(8,128)S(1)} %collective-permute-done.refs_0_, f32[2,128,128]{2,1,0:T(8,128)S(1)} %collective-permute-done.1.refs_1_, f32[1,128,128]{2,1,0:T(8,128)S(1)} %collective-permute-done.2.refs_2_, f32[2,128,128]{2,1,0:T(8,128)S(1)} %collective-permute-done.4.refs_3_, ...), custom_call_target="tpu_custom_call" | custom-call | tf_op jit(solution)/shard_map/weights/pallas_call | solution.py:289
  173.9 2.1 %beams.3 = bf16[8,2048,256]{2,1,0:T(8,128)(2,1)} custom-call(bf16[3,256,256]{2,1,0:T(8,128)(2,1)S(1)} %weights.2.w_ref, bf16[3,2048,256]{2,1,0:T(8,128)(2,1)S(1)} %compress.2.z_in, bf16[8,2048,256]{2,1,0:T(8,128)(2,1)} %beams.2.refs_0_), custom_call_target="tpu_custom_call", output_to_operand_aliasing={{}: (2, {})} | custom-call | tf_op jit(solution)/shard_map/beams/pallas_call | solution.py:431
  (19 shorter events, 0.1 us)
Async XLA Ops:
  7.8 74.3 %all-to-all-start = ((bf16[32,5,64,256]{3,2,1,0:T(8,128)(2,1)}), bf16[32,5,64,256]{3,2,1,0:T(8,128)(2,1)}, u32[]{:S(2)}, u32[]{:S(2)}) async-start(bf16[32,5,64,256]{3,2,1,0:T(8,128)(2,1)} %bitcast.23), calls=%async_computation | async-start | bytes 10485760 | tf_op jit(solution)/shard_map/all_to_all | solution.py:459
  23.3 62.9 %copy-start.2 = (s32[1,8,6]{1,0,2:T(1,128)S(1)}, s32[1,8,6]{1,0,2:T(1,128)}, u32[]{:S(2)}) copy-start(s32[1,8,6]{1,0,2:T(1,128)} %param.6) | copy-start | bytes 580
  23.3 62.9 %copy-start.1 = (s32[1,8]{1,0:T(1,128)S(1)}, s32[1,8]{1,0:T(1,128)}, u32[]{:S(2)}) copy-start(s32[1,8]{1,0:T(1,128)} %param.7) | copy-start | bytes 100
  82.1 46.1 %all-to-all-start.1 = ((bf16[32,3,64,256]{3,2,1,0:T(8,128)(2,1)}), bf16[32,3,64,256]{3,2,1,0:T(8,128)(2,1)S(1)}, u32[]{:S(2)}, u32[]{:S(2)}) async-start(bf16[32,3,64,256]{3,2,1,0:T(8,128)(2,1)} %bitcast.24), calls=%async_computation.1 | async-start | bytes 6291456 | tf_op jit(solution)/shard_map/all_to_all | solution.py:459
  86.2 46.8 %copy-start.3 = (f32[64]{0:T(128)S(1)}, f32[64]{0:T(128)}, u32[]{:S(2)}) copy-start(f32[64]{0:T(128)} %param.9) | copy-start | bytes 772
  89.3 7.2 %collective-permute-start.6 = (f32[2,128,128]{2,1,0:T(8,128)}, f32[2,128,128]{2,1,0:T(8,128)}, u32[]{:S(2)}, u32[]{:S(2)}) collective-permute-start(f32[2,128,128]{2,1,0:T(8,128)} %get-tuple-element.19), channel_id=1, source_target_pairs={{0,32},{32,64},{64,96},{96,0},{1,33},{33,65},{65,97},{97,1},{2,34}... | collective-permute-start | bytes 393224 | tf_op jit(solution)/shard_map/ppermute | solution.py:34
  90.9 42.1 %collective-permute-start.11 = (f32[2,128,128]{2,1,0:T(8,128)}, f32[2,128,128]{2,1,0:T(8,128)}, u32[]{:S(2)}, u32[]{:S(2)}) collective-permute-start(f32[2,128,128]{2,1,0:T(8,128)} %get-tuple-element.19), channel_id=1, source_target_pairs={{0,96},{32,0},{64,32},{96,64},{1,97},{33,1},{65,33},{97,65},{2,98}... | collective-permute-start | bytes 393224 | tf_op jit(solution)/shard_map/ppermute | solution.py:34
  92.6 40.6 %collective-permute-start.9 = (f32[3,128,128]{2,1,0:T(8,128)}, f32[3,128,128]{2,1,0:T(8,128)S(1)}, u32[]{:S(2)}, u32[]{:S(2)}) collective-permute-start(f32[3,128,128]{2,1,0:T(8,128)} %get-tuple-element.20), channel_id=1, source_target_pairs={{0,96},{32,0},{64,32},{96,64},{1,97},{33,1},{65,33},{97,65},{2,98}... | collective-permute-start | bytes 589832 | tf_op jit(solution)/shard_map/ppermute | solution.py:34
  94.4 42.0 %collective-permute-start.7 = (f32[3,128,128]{2,1,0:T(8,128)}, f32[3,128,128]{2,1,0:T(8,128)S(1)}, u32[]{:S(2)}, u32[]{:S(2)}) collective-permute-start(f32[3,128,128]{2,1,0:T(8,128)} %get-tuple-element.20), channel_id=1, source_target_pairs={{0,32},{32,64},{64,96},{96,0},{1,33},{33,65},{65,97},{97,1},{2,34}... | collective-permute-start | bytes 589832 | tf_op jit(solution)/shard_map/ppermute | solution.py:34
  96.5 40.0 %collective-permute-start.8 = (f32[2,128,128]{2,1,0:T(8,128)}, f32[2,128,128]{2,1,0:T(8,128)}, u32[]{:S(2)}, u32[]{:S(2)}) collective-permute-start(f32[2,128,128]{2,1,0:T(8,128)} %collective-permute-done.6.refs_0_), channel_id=1, source_target_pairs={{0,32},{32,64},{64,96},{96,0},{1,33},{33,65},{65,97},{97,1},{2,34}... | collective-permute-start | bytes 393224 | tf_op jit(solution)/shard_map/ppermute | solution.py:34
  129.9 9.4 %collective-permute-start.3 = (f32[2,128,128]{2,1,0:T(8,128)S(1)}, f32[2,128,128]{2,1,0:T(8,128)S(1)}, u32[]{:S(2)}, u32[]{:S(2)}) collective-permute-start(f32[2,128,128]{2,1,0:T(8,128)S(1)} %get-tuple-element.16), channel_id=1, source_target_pairs={{0,96},{32,0},{64,32},{96,64},{1,97},{33,1},{65,33},{97,65},{2,98}... | collective-permute-start | bytes 393224 | tf_op jit(solution)/shard_map/ppermute | solution.py:34
  133.0 6.2 %collective-permute-start = (f32[1,128,128]{2,1,0:T(8,128)S(1)}, f32[1,128,128]{2,1,0:T(8,128)S(1)}, u32[]{:S(2)}, u32[]{:S(2)}) collective-permute-start(f32[1,128,128]{2,1,0:T(8,128)S(1)} %get-tuple-element.15), channel_id=1, source_target_pairs={{0,32},{32,64},{64,96},{96,0},{1,33},{33,65},{65,97},{97,1},{2,34}... | collective-permute-start | bytes 196616 | tf_op jit(solution)/shard_map/ppermute | solution.py:34
  133.1 17.9 %collective-permute-start.10 = (f32[3,128,128]{2,1,0:T(8,128)S(1)}, f32[3,128,128]{2,1,0:T(8,128)S(1)}, u32[]{:S(2)}, u32[]{:S(2)}) collective-permute-start(f32[3,128,128]{2,1,0:T(8,128)S(1)} %collective-permute-done.9.refs_5_), channel_id=1, source_target_pairs={{0,96},{32,0},{64,32},{96,64},{1,97},{33,1},{65,33},{97,65},{2,98}... | collective-permute-start | bytes 589832 | tf_op jit(solution)/shard_map/ppermute | solution.py:34
  136.4 32.6 %collective-permute-start.5 = (f32[1,128,128]{2,1,0:T(8,128)S(1)}, f32[1,128,128]{2,1,0:T(8,128)S(1)}, u32[]{:S(2)}, u32[]{:S(2)}) collective-permute-start(f32[1,128,128]{2,1,0:T(8,128)S(1)} %get-tuple-element.15), channel_id=1, source_target_pairs={{0,96},{32,0},{64,32},{96,64},{1,97},{33,1},{65,33},{97,65},{2,98}... | collective-permute-start | bytes 196616 | tf_op jit(solution)/shard_map/ppermute | solution.py:34
  136.5 32.5 %collective-permute-start.1 = (f32[2,128,128]{2,1,0:T(8,128)S(1)}, f32[2,128,128]{2,1,0:T(8,128)S(1)}, u32[]{:S(2)}, u32[]{:S(2)}) collective-permute-start(f32[2,128,128]{2,1,0:T(8,128)S(1)} %get-tuple-element.16), channel_id=1, source_target_pairs={{0,32},{32,64},{64,96},{96,0},{1,33},{33,65},{65,97},{97,1},{2,34}... | collective-permute-start | bytes 393224 | tf_op jit(solution)/shard_map/ppermute | solution.py:34
  139.3 29.8 %collective-permute-start.2 = (f32[1,128,128]{2,1,0:T(8,128)S(1)}, f32[1,128,128]{2,1,0:T(8,128)S(1)}, u32[]{:S(2)}, u32[]{:S(2)}) collective-permute-start(f32[1,128,128]{2,1,0:T(8,128)S(1)} %collective-permute-done.refs_0_), channel_id=1, source_target_pairs={{0,32},{32,64},{64,96},{96,0},{1,33},{33,65},{65,97},{97,1},{2,34}... | collective-permute-start | bytes 196616 | tf_op jit(solution)/shard_map/ppermute | solution.py:34
  139.3 29.8 %collective-permute-start.4 = (f32[2,128,128]{2,1,0:T(8,128)S(1)}, f32[2,128,128]{2,1,0:T(8,128)S(1)}, u32[]{:S(2)}, u32[]{:S(2)}) collective-permute-start(f32[2,128,128]{2,1,0:T(8,128)S(1)} %collective-permute-done.3.refs_5_), channel_id=1, source_target_pairs={{0,96},{32,0},{64,32},{96,64},{1,97},{33,1},{65,33},{97,65},{2,98}... | collective-permute-start | bytes 393224 | tf_op jit(solution)/shard_map/ppermute | solution.py:34
  159.1 0.9 copy-start
where the time goes:
time: 177 us; the launch traced here: 176 us
  waiting for transfers between devices  92.8 us (52%)
  Pallas kernels  49.5 us (28%)
  starting transfers between devices  29.8 us (17%)
  matrix products  2.64 us (1%)
    all_to_all x2, waiting for transfers between devices, chain(): lax.all_to_all(sent, 'blk', split_axis=0, concat_axis=0, tiled=True)  90.1 us
    ppermute x12, starting transfers between devices, shifted(): lax.ppermute(x, 'segment', [(i, (i + by) % peers) for i in range(peers)])  17.3 us
    pallas_call x2, Pallas kernels, doppler(): pl.pallas_call(make_doppler_kernel(owners, first, count), out_shape=pltpu...  14.9 us
    pallas_call x2, Pallas kernels, beam_weights(): pl.pallas_call(weights_kernel, out_shape=jax.ShapeDtypeStruct((count, 2 *...  12.9 us
    all_to_all x2, starting transfers between devices, chain(): lax.all_to_all(sent, 'blk', split_axis=0, concat_axis=0, tiled=True)  12.5 us
    pallas_call x2, Pallas kernels, form_beams(): pl.pallas_call(make_beams_kernel(first, len(aliases)), out_shape=jax.Shap...  8.72 us
    pallas_call x2, Pallas kernels, compress(): pl.pallas_call(compress_kernel, out_shape=pltpu.HBM(shape, bf16) if count...  8.28 us
    pallas_call x2, Pallas kernels, covariance(): pl.pallas_call(make_cov_kernel(first, count, listed), out_shape=[jax.Shap...  4.72 us
  transfers between devices with their start and end apart: 14, of which 4 were waited for; matrix products, arithmetic and copies ran while one was open for 2% of the time, Pallas kernels for 20%

commit v1 on v0

--- a/solution.py
+++ b/solution.py
@@ -14,8 +14,8 @@
 NTR_EASY = 3
 NS_STEPS = 12
 CBLK = 128
-CHUNKS = (5, 3)
-RESIDENT = 3
+CHUNKS = (6, 2)
+EARLY = 2
 
 decay_rate = 0.7
 diag_load = 0.1
@@ -320,86 +320,65 @@
     return table.astype(bf16).reshape(2 * block_len, 2 * block_len)
 
 
-def compress_kernel(table_ref, y_hbm, z_out, y_ref, in_sem, *held):
-    count, sources, per, _ = y_ref.shape
-    z_ref, out_sem = held if held else (z_out, None)
+def compress_rows(table_ref, y_ref, z_ref):
+    sources, per, _ = y_ref.shape
     step = CBLK // per
     half = CH
-
+    for start in range(0, sources, step):
+        stop = min(start + 2 * step, sources)
+        y = y_ref[start:stop].reshape((stop - start) * per, 2 * half)
+        m = jnp.dot(table_ref[:, : y.shape[0]], y, preferred_element_type=f32)
+        r = pl.ds(start * per, CBLK)
+        z_ref[r, :half] = (m[:CBLK, :half] + m[CBLK:, half:]).astype(bf16)
+        z_ref[r, half:] = (m[:CBLK, half:] - m[CBLK:, :half]).astype(bf16)
+
+
+def compress_kernel(table_ref, y_hbm, z_ref, y_ref, sem):
     def load(i):
-        return pltpu.make_async_copy(y_hbm.at[:, i], y_ref.at[i], in_sem.at[i])
-
-    def save(i):
-        return pltpu.make_async_copy(z_ref.at[i], z_out.at[i], out_sem.at[i])
-
+        return pltpu.make_async_copy(y_hbm.at[:, i], y_ref.at[i], sem.at[i])
+
+    count = y_ref.shape[0]
     for i in range(count):
         load(i).start()
     for i in range(count):
         load(i).wait()
-        for start in range(0, sources, step):
-            stop = min(start + 2 * step, sources)
-            y = y_ref[i, start:stop].reshape((stop - start) * per, 2 * half)
-            m = jnp.dot(table_ref[:, : y.shape[0]], y, preferred_element_type=f32)
-            r = pl.ds(start * per, CBLK)
-            z_ref[i, r, :half] = (m[:CBLK, :half] + m[CBLK:, half:]).astype(bf16)
-            z_ref[i, r, half:] = (m[:CBLK, half:] - m[CBLK:, :half]).astype(bf16)
-        if held:
-            save(i).start()
-    if held:
-        for i in range(count):
-            save(i).wait()
+        compress_rows(table_ref, y_ref.at[i], z_ref.at[i])
 
 
 def compress(owned, table):
     sources, count, per, width = owned.shape
     vmem = pl.BlockSpec(memory_space=pltpu.VMEM)
-    anywhere = pl.BlockSpec(memory_space=pl.ANY)
-    shape = (count, sources * per, width)
-    scratch = [
-        pltpu.VMEM((count, sources, per, width), bf16),
-        pltpu.SemaphoreType.DMA((count,)),
-    ]
-    if count > RESIDENT:
-        scratch += [pltpu.VMEM(shape, bf16), pltpu.SemaphoreType.DMA((count,))]
     return pl.pallas_call(
         compress_kernel,
-        out_shape=pltpu.HBM(shape, bf16) if count > RESIDENT else jax.ShapeDtypeStruct(shape, bf16),
-        in_specs=[vmem, anywhere],
-        out_specs=anywhere if count > RESIDENT else vmem,
-        scratch_shapes=scratch,
+        out_shape=jax.ShapeDtypeStruct((count, sources * per, width), bf16),
+        in_specs=[vmem, pl.BlockSpec(memory_space=pl.ANY)],
+        out_specs=vmem,
+        scratch_shapes=[
+            pltpu.VMEM((count, sources, per, width), bf16),
+            pltpu.SemaphoreType.DMA((count,)),
+        ],
         compiler_params=params(32),
         name="compress",
     )(table, owned)
 
 
 def make_beams_kernel(first, aliased):
-    def beams_kernel(w_ref, z_in, *refs):
-        o_hbm, o_ref, out_sem, *held = refs[aliased:]
-        z_ref, in_sem = held if held else (z_in, None)
+    def beams_kernel(w_ref, z_ref, *refs):
+        o_hbm, o_ref, sem = refs[aliased:]
         count, rows, _ = z_ref.shape
-        pieces = out_sem.shape[1]
+        pieces = sem.shape[1]
         step = rows // pieces
 
-        def load(i):
-            return pltpu.make_async_copy(z_in.at[i], z_ref.at[i], in_sem.at[i])
-
         def save(i, p):
-            piece = pl.ds(p * step, step)
-            return pltpu.make_async_copy(
-                o_ref.at[i, piece], o_hbm.at[first + i, piece], out_sem.at[i, p]
-            )
-
-        if held:
-            for i in range(count):
-                load(i).start()
-        for i in range(count):
-            if held:
-                load(i).wait()
+            r = pl.ds(p * step, step)
+            return pltpu.make_async_copy(o_ref.at[i, r], o_hbm.at[first + i, r], sem.at[i, p])
+
+        for i in range(count):
             for p in range(pieces):
                 r = pl.ds(p * step, step)
-                o_ref[i, r] = jnp.dot(
-                    z_ref[i, r], w_ref[i], preferred_element_type=f32
-                ).astype(bf16)
+                o_ref[i, r] = jnp.dot(z_ref[i, r], w_ref[i], preferred_element_type=f32).astype(
+                    bf16
+                )
                 save(i, p).start()
         for i in range(count):
             for p in range(pieces):
@@ -411,33 +390,71 @@
 def form_beams(z, weights, held, bins, first):
     count, rows, _ = z.shape
     width = weights.shape[2]
-    resident = count <= RESIDENT
     vmem = pl.BlockSpec(memory_space=pltpu.VMEM)
     anywhere = pl.BlockSpec(memory_space=pl.ANY)
-    in_specs = [vmem, vmem if resident else anywhere]
-    operands = [weights, z]
-    aliases = {}
-    if held is not None:
-        in_specs.append(anywhere)
-        operands.append(held)
-        aliases = {2: 0}
-    pieces = 2 if resident else 1
-    scratch = [
-        pltpu.VMEM((count, rows, width), bf16),
-        pltpu.SemaphoreType.DMA((count, pieces)),
-    ]
-    if not resident:
-        scratch += [pltpu.VMEM(z.shape, bf16), pltpu.SemaphoreType.DMA((count,))]
+    before = [] if held is None else [held]
     return pl.pallas_call(
-        make_beams_kernel(first, len(aliases)),
+        make_beams_kernel(first, len(before)),
         out_shape=jax.ShapeDtypeStruct((bins, rows, width), bf16),
-        in_specs=in_specs,
+        in_specs=[vmem, vmem] + [anywhere] * len(before),
         out_specs=anywhere,
-        scratch_shapes=scratch,
-        input_output_aliases=aliases,
-        compiler_params=params(32 if resident else 59),
+        scratch_shapes=[
+            pltpu.VMEM((count, rows, width), bf16),
+            pltpu.SemaphoreType.DMA((count, 2)),
+        ],
+        input_output_aliases={2: 0} if before else {},
+        compiler_params=params(32),
         name="beams",
-    )(*operands)
+    )(weights, z, *before)
+
+
+def make_returns_kernel(first, skip, aliased):
+    def returns_kernel(table_ref, w_ref, y_hbm, *refs):
+        o_hbm, y_ref, z_ref, o_ref, in_sem, out_sem = refs[aliased:]
+        count = y_ref.shape[0]
+
+        def load(i):
+            return pltpu.make_async_copy(y_hbm.at[:, skip + i], y_ref.at[i], in_sem.at[i])
+
+        def save(i):
+            return pltpu.make_async_copy(o_ref.at[i], o_hbm.at[first + skip + i], out_sem.at[i])
+
+        for i in range(count):
+            load(i).start()
+        for i in range(count):
+            load(i).wait()
+            compress_rows(table_ref, y_ref.at[i], z_ref.at[i])
+            o_ref[i] = jnp.dot(z_ref[i], w_ref[skip + i], preferred_element_type=f32).astype(bf16)
+            save(i).start()
+        for i in range(count):
+            save(i).wait()
+
+    return returns_kernel
+
+
+def form_returns(owned, table, weights, held, bins, first, skip, count):
+    sources, _, per, _ = owned.shape
+    width = weights.shape[2]
+    rows = sources * per
+    vmem = pl.BlockSpec(memory_space=pltpu.VMEM)
+    anywhere = pl.BlockSpec(memory_space=pl.ANY)
+    before = [] if held is None else [held]
+    return pl.pallas_call(
+        make_returns_kernel(first, skip, len(before)),
+        out_shape=jax.ShapeDtypeStruct((bins, rows, width), bf16),
+        in_specs=[vmem, vmem, anywhere] + [anywhere] * len(before),
+        out_specs=anywhere,
+        scratch_shapes=[
+            pltpu.VMEM((count, sources, per, owned.shape[3]), bf16),
+            pltpu.VMEM((count, rows, owned.shape[3]), bf16),
+            pltpu.VMEM((count, rows, width), bf16),
+            pltpu.SemaphoreType.DMA((count,)),
+            pltpu.SemaphoreType.DMA((count,)),
+        ],
+        input_output_aliases={3: 0} if before else {},
+        compiler_params=params(59),
+        name="returns",
+    )(table, weights, owned, *before)
 
 
 def chain(echoes, train_blocks, hard_bins, owner_map, code_phase):
@@ -458,13 +475,17 @@
             sent, owned[-1] = lax.optimization_barrier((sent, owned[-1]))
         owned.append(lax.all_to_all(sent, "blk", split_axis=0, concat_axis=0, tiled=True))
     result = None
-    for first, y in zip(firsts, owned):
+    for g, (first, y) in enumerate(zip(firsts, owned)):
         count = y.shape[1]
         pieces = [count // 2, count - count // 2] if count > 2 else [count]
         parts = earlier(covariance(y, blocks, hard, first, pieces))
-        z = compress(y, table)
+        if g == len(CHUNKS) - 1:
+            z = compress(y, table)
+            result = form_beams(z, beam_weights(parts), result, bins, first)
+            continue
         weights = beam_weights(parts)
-        result = form_beams(z, weights, result, bins, first)
+        for skip, some in ((0, EARLY), (EARLY, count - EARLY)):
+            result = form_returns(y, table, weights, result, bins, first, skip, some)
     return result[None]
 
 

time: 177 us -> 172 us (0.972)
  waiting for transfers between devices: 92.8 us -> 86.4 us
  local copies, waits for them, and re-layouts: 1.02 us -> 3.05 us
  starting transfers between devices: 29.8 us -> 27.9 us
    all_to_all x2, waiting for transfers between devices: 90.1 us -> 77.4 us  [chain(): lax.all_to_all(sent, 'blk', split_axis=0, concat_axis=0, tiled=True)]
    ppermute x12 -> x9, waiting for transfers between devices: 2.73 us -> 9.04 us  [shifted(): lax.ppermute(x, 'segment', [(i, (i + by) % peers) for i in range(peers)])]
    ppermute x12 -> x9, starting transfers between devices: 17.3 us -> 15.5 us  [shifted(): lax.ppermute(x, 'segment', [(i, (i + by) % peers) for i in range(peers)])]
  transfers between devices with their start and end apart: 14 -> 11, of which waited for: 4 -> 3; matrix products, arithmetic and copies ran while one was open for 2% -> 3% of each run, Pallas kernels for 20% -> 20%
where the time goes in v1:
time: 172 us
  waiting for transfers between devices  86.4 us (50%)
  Pallas kernels  50.1 us (29%)
  starting transfers between devices  27.9 us (16%)
  matrix products  3.55 us (2%)
  local copies, waits for them, and re-layouts  3.05 us (2%)
    all_to_all x2, waiting for transfers between devices, chain(): lax.all_to_all(sent, 'blk', split_axis=0, concat_axis=0, tiled=True)  77.4 us
    ppermute x9, starting transfers between devices, shifted(): lax.ppermute(x, 'segment', [(i, (i + by) % peers) for i in range(peers)])  15.5 us
    pallas_call x2, Pallas kernels, doppler(): pl.pallas_call(make_doppler_kernel(owners, first, count), out_shape=pltpu...  15.4 us
    pallas_call x2, Pallas kernels, form_returns(): pl.pallas_call(make_returns_kernel(first, skip, len(before)), out_shape=j...  14 us
    pallas_call x2, Pallas kernels, beam_weights(): pl.pallas_call(weights_kernel, out_shape=jax.ShapeDtypeStruct((count, 2 *...  12.8 us
    all_to_all x2, starting transfers between devices, chain(): lax.all_to_all(sent, 'blk', split_axis=0, concat_axis=0, tiled=True)  12.4 us
    ppermute x9, waiting for transfers between devices, shifted(): lax.ppermute(x, 'segment', [(i, (i + by) % peers) for i in range(peers)])  9.04 us
    pallas_call x2, Pallas kernels, covariance(): pl.pallas_call(make_cov_kernel(first, count, listed), out_shape=[jax.Shap...  4.53 us
  transfers between devices with their start and end apart: 11, of which 3 were waited for; matrix products, arithmetic and copies ran while one was open for 3% of the time, Pallas kernels for 20%

profile of v1, /device:TPU:0, one launch (start us, length us, event | category | flops | bytes accessed | tf_op | source)
XLA Modules:
  0.0 172.0 jit_solution(13645247075038839998)
XLA Ops:
  0.0 8.7 %doppler.3 = bf16[192,64,256]{2,1,0:T(8,128)(2,1)} custom-call(s32[1,256]{1,0:T(1,128)} %bitcast.26, bf16[64,128,512]{2,1,0:T(8,128)(2,1)} %bitcast.22), custom_call_target="tpu_custom_call" | custom-call | tf_op jit(solution)/shard_map/doppler/pallas_call | solution.py:123
  8.7 8.4 %all-to-all-start = ((bf16[32,6,64,256]{3,2,1,0:T(8,128)(2,1)}), bf16[32,6,64,256]{3,2,1,0:T(8,128)(2,1)}, u32[]{:S(2)}, u32[]{:S(2)}) async-start(bf16[32,6,64,256]{3,2,1,0:T(8,128)(2,1)} %bitcast.24), calls=%async_computation | async-start | bytes 12582912 | tf_op jit(solution)/shard_map/all_to_all | solution.py:476
  17.1 6.7 %doppler.2 = bf16[64,64,256]{2,1,0:T(8,128)(2,1)} custom-call(s32[1,256]{1,0:T(1,128)} %bitcast.27, bf16[64,128,512]{2,1,0:T(8,128)(2,1)} %bitcast.23), custom_call_target="tpu_custom_call" | custom-call | tf_op jit(solution)/shard_map/doppler/pallas_call | solution.py:123
  23.8 0.0 copy-start.4
  23.8 0.0 copy-start.3
  23.9 71.1 %all-to-all-done.y_ref.y_hbm = bf16[32,6,64,256]{3,2,1,0:T(8,128)(2,1)} async-done(((bf16[32,6,64,256]{3,2,1,0:T(8,128)(2,1)}), bf16[32,6,64,256]{3,2,1,0:T(8,128)(2,1)}, u32[]{:S(2)}, u32[]{:S(2)}) %all-to-all-start) | async-done | bytes 6291488 | tf_op jit(solution)/shard_map/all_to_all | solution.py:476
  95.0 4.0 %all-to-all-start.1 = ((bf16[32,2,64,256]{3,2,1,0:T(8,128)(2,1)}), bf16[32,2,64,256]{3,2,1,0:T(8,128)(2,1)S(1)}, u32[]{:S(2)}, u32[]{:S(2)}) async-start(bf16[32,2,64,256]{3,2,1,0:T(8,128)(2,1)} %bitcast.25), calls=%async_computation.1 | async-start | bytes 4194304 | tf_op jit(solution)/shard_map/all_to_all | solution.py:476
  99.0 0.8 copy.8
  99.8 0.7 iota_subtract_fusion
  100.4 0.7 copy-done.2
  101.1 3.1 %covariance.3 = (f32[3,128,128]{2,1,0:T(8,128)S(1)}, f32[3,128,128]{2,1,0:T(8,128)}) custom-call(s32[8,6]{1,0:T(8,128)S(1)} %bitcast.18, s32[8]{0:T(128)S(1)} %bitcast.20, bf16[32,6,64,256]{3,2,1,0:T(8,128)(2,1)} %all-to-all-done.y_ref.y_hbm), custom_call_target="tpu_custom_call" | custom-call | tf_op jit(solution)/shard_map/covariance/pallas_call | solution.py:193
  104.2 3.1 %collective-permute-start.6 = (f32[3,128,128]{2,1,0:T(8,128)}, f32[3,128,128]{2,1,0:T(8,128)S(1)}, u32[]{:S(2)}, u32[]{:S(2)}) collective-permute-start(f32[3,128,128]{2,1,0:T(8,128)} %get-tuple-element.16), channel_id=1, source_target_pairs={{0,96},{32,0},{64,32},{96,64},{1,97},{33,1},{65,33},{97,65},{2,98}... | collective-permute-start | bytes 589832 | tf_op jit(solution)/shard_map/ppermute | solution.py:34
  107.3 0.6 collective-permute-start.3
  107.9 2.7 %collective-permute-start.8 = (f32[3,128,128]{2,1,0:T(8,128)S(1)}, f32[3,128,128]{2,1,0:T(8,128)S(1)}, u32[]{:S(2)}, u32[]{:S(2)}) collective-permute-start(f32[3,128,128]{2,1,0:T(8,128)S(1)} %get-tuple-element.15), channel_id=1, source_target_pairs={{0,96},{32,0},{64,32},{96,64},{1,97},{33,1},{65,33},{97,65},{2,98}... | collective-permute-start | bytes 589832 | tf_op jit(solution)/shard_map/ppermute | solution.py:34
  110.6 9.0 %collective-permute-done.3.refs_0_ = f32[3,128,128]{2,1,0:T(8,128)S(1)} collective-permute-done((f32[3,128,128]{2,1,0:T(8,128)S(1)}, f32[3,128,128]{2,1,0:T(8,128)S(1)}, u32[]{:S(2)}, u32[]{:S(2)}) %collective-permute-start.3) | collective-permute-done | bytes 196640 | tf_op jit(solution)/shard_map/ppermute | solution.py:34
  119.6 0.0 collective-permute-start.5
  119.6 0.0 collective-permute-done.6.refs_5_
  119.6 3.2 %collective-permute-start.7 = (f32[3,128,128]{2,1,0:T(8,128)S(1)}, f32[3,128,128]{2,1,0:T(8,128)S(1)}, u32[]{:S(2)}, u32[]{:S(2)}) collective-permute-start(f32[3,128,128]{2,1,0:T(8,128)S(1)} %collective-permute-done.6.refs_5_), channel_id=1, source_target_pairs={{0,96},{32,0},{64,32},{96,64},{1,97},{33,1},{65,33},{97,65},{2,98}... | collective-permute-start | bytes 589832 | tf_op jit(solution)/shard_map/ppermute | solution.py:34
  122.9 6.2 %all-to-all-done.1.y_ref.y_hbm = bf16[32,2,64,256]{3,2,1,0:T(8,128)(2,1)S(1)} async-done(((bf16[32,2,64,256]{3,2,1,0:T(8,128)(2,1)}), bf16[32,2,64,256]{3,2,1,0:T(8,128)(2,1)S(1)}, u32[]{:S(2)}, u32[]{:S(2)}) %all-to-all-start.1) | async-done | bytes 2097184 | tf_op jit(solution)/shard_map/all_to_all | solution.py:476
  129.1 1.4 covariance.2
  130.5 1.6 collective-permute-start
  132.2 2.9 %collective-permute-start.1 = (f32[2,128,128]{2,1,0:T(8,128)S(1)}, f32[2,128,128]{2,1,0:T(8,128)S(1)}, u32[]{:S(2)}, u32[]{:S(2)}) collective-permute-start(f32[2,128,128]{2,1,0:T(8,128)S(1)} %covariance.2), channel_id=1, source_target_pairs={{0,64},{32,96},{64,0},{96,32},{1,65},{33,97},{65,1},{97,33},{2,66}... | collective-permute-start | bytes 393224 | tf_op jit(solution)/shard_map/ppermute | solution.py:34
  135.1 1.3 collective-permute-start.2
  136.4 3.5 %fusion.2 = bf16[2,128,256]{2,0,1:T(2,128)(2,1)S(1)} fusion(s32[128,256]{1,0:T(8,128)} %iota_subtract_fusion, f32[1,64]{1,0:T(1,128)S(1)} %get-tuple-element.18, f32[1,64]{1,0:T(1,128)S(1)} %get-tuple-element.17), kind=kOutput, calls=%fused_computation.3 | convolution fusion | flops 52494592 | bytes 262656 | tf_op jit(solution)/shard_map/pql,kl->kpq/dot_general | solution.py:319
  140.0 0.7 copy.9
  140.7 7.8 %weights.3.w_ref = bf16[6,256,256]{2,1,0:T(8,128)(2,1)S(1)} custom-call(f32[3,128,128]{2,1,0:T(8,128)S(1)} %collective-permute-done.3.refs_0_, f32[3,128,128]{2,1,0:T(8,128)S(1)} %collective-permute-done.4.refs_1_, f32[3,128,128]{2,1,0:T(8,128)S(1)} %collective-permute-done.5.refs_2_, f32[3,128,128]{2,1,0:T(8,128)S(1)} %collective-permute-done.7.refs_3_, ...), custom_call_target="tpu_custom_call" | custom-call | tf_op jit(solution)/shard_map/weights/pallas_call | solution.py:289
  148.5 0.9 copy-done
  149.4 5.9 %returns.2.refs_0_ = bf16[8,2048,256]{2,1,0:T(8,128)(2,1)} custom-call(bf16[256,256]{1,0:T(8,128)(2,1)} %bitcast.15, bf16[6,256,256]{2,1,0:T(8,128)(2,1)} %copy-done, bf16[32,6,64,256]{3,2,1,0:T(8,128)(2,1)} %all-to-all-done.y_ref.y_hbm), custom_call_target="tpu_custom_call" | custom-call | tf_op jit(solution)/shard_map/returns/pallas_call | solution.py:442
  155.3 8.1 %returns.3.refs_0_ = bf16[8,2048,256]{2,1,0:T(8,128)(2,1)} custom-call(bf16[256,256]{1,0:T(8,128)(2,1)} %bitcast.16, bf16[6,256,256]{2,1,0:T(8,128)(2,1)} %copy-done, bf16[32,6,64,256]{3,2,1,0:T(8,128)(2,1)} %all-to-all-done.y_ref.y_hbm, bf16[8,2048,256]{2,1,0:T(8,128)(2,1)} %returns.2.refs_0_), custom_call_target="tpu_custom_call", output_to_operand_aliasing={{}: (3, {})} | custom-call | tf_op jit(solution)/shard_map/returns/pallas_call | solution.py:442
  163.4 1.6 compress.1.z_ref
  165.1 5.0 %weights.2.w_ref = bf16[2,256,256]{2,1,0:T(8,128)(2,1)S(1)} custom-call(f32[2,128,128]{2,1,0:T(8,128)S(1)} %collective-permute-done.refs_0_, f32[2,128,128]{2,1,0:T(8,128)S(1)} %collective-permute-done.1.refs_1_, f32[2,128,128]{2,1,0:T(8,128)S(1)} %collective-permute-done.2.refs_2_), custom_call_target="tpu_custom_call" | custom-call | tf_op jit(solution)/shard_map/weights/pallas_call | solution.py:289
  170.0 1.8 %beams.1 = bf16[8,2048,256]{2,1,0:T(8,128)(2,1)} custom-call(bf16[2,256,256]{2,1,0:T(8,128)(2,1)S(1)} %weights.2.w_ref, bf16[2,2048,256]{2,1,0:T(8,128)(2,1)S(1)} %compress.1.z_ref, bf16[8,2048,256]{2,1,0:T(8,128)(2,1)} %returns.3.refs_0_), custom_call_target="tpu_custom_call", output_to_operand_aliasing={{}: (2, {})} | custom-call | tf_op jit(solution)/shard_map/beams/pallas_call | solution.py:396
  (15 shorter events, 0.1 us)
Async XLA Ops:
  8.7 86.3 %all-to-all-start = ((bf16[32,6,64,256]{3,2,1,0:T(8,128)(2,1)}), bf16[32,6,64,256]{3,2,1,0:T(8,128)(2,1)}, u32[]{:S(2)}, u32[]{:S(2)}) async-start(bf16[32,6,64,256]{3,2,1,0:T(8,128)(2,1)} %bitcast.24), calls=%async_computation | async-start | bytes 12582912 | tf_op jit(solution)/shard_map/all_to_all | solution.py:476
  23.8 86.7 %copy-start.4 = (f32[64]{0:T(128)S(1)}, f32[64]{0:T(128)}, u32[]{:S(2)}) copy-start(f32[64]{0:T(128)} %param.9) | copy-start | bytes 772
  23.8 105.3 %copy-start.3 = (s32[1,8]{1,0:T(1,128)S(1)}, s32[1,8]{1,0:T(1,128)}, u32[]{:S(2)}) copy-start(s32[1,8]{1,0:T(1,128)} %param.7) | copy-start | bytes 100
  95.0 34.1 %all-to-all-start.1 = ((bf16[32,2,64,256]{3,2,1,0:T(8,128)(2,1)}), bf16[32,2,64,256]{3,2,1,0:T(8,128)(2,1)S(1)}, u32[]{:S(2)}, u32[]{:S(2)}) async-start(bf16[32,2,64,256]{3,2,1,0:T(8,128)(2,1)} %bitcast.25), calls=%async_computation.1 | async-start | bytes 4194304 | tf_op jit(solution)/shard_map/all_to_all | solution.py:476
  100.4 0.7 copy-start.2
  104.2 15.4 %collective-permute-start.6 = (f32[3,128,128]{2,1,0:T(8,128)}, f32[3,128,128]{2,1,0:T(8,128)S(1)}, u32[]{:S(2)}, u32[]{:S(2)}) collective-permute-start(f32[3,128,128]{2,1,0:T(8,128)} %get-tuple-element.16), channel_id=1, source_target_pairs={{0,96},{32,0},{64,32},{96,64},{1,97},{33,1},{65,33},{97,65},{2,98}... | collective-permute-start | bytes 589832 | tf_op jit(solution)/shard_map/ppermute | solution.py:34
  107.3 24.9 %collective-permute-start.4 = (f32[3,128,128]{2,1,0:T(8,128)}, f32[3,128,128]{2,1,0:T(8,128)S(1)}, u32[]{:S(2)}, u32[]{:S(2)}) collective-permute-start(f32[3,128,128]{2,1,0:T(8,128)} %get-tuple-element.16), channel_id=1, source_target_pairs={{0,32},{32,64},{64,96},{96,0},{1,33},{33,65},{65,97},{97,1},{2,34}... | collective-permute-start | bytes 589832 | tf_op jit(solution)/shard_map/ppermute | solution.py:34
  107.3 12.3 %collective-permute-start.3 = (f32[3,128,128]{2,1,0:T(8,128)S(1)}, f32[3,128,128]{2,1,0:T(8,128)S(1)}, u32[]{:S(2)}, u32[]{:S(2)}) collective-permute-start(f32[3,128,128]{2,1,0:T(8,128)S(1)} %get-tuple-element.15), channel_id=1, source_target_pairs={{0,32},{32,64},{64,96},{96,0},{1,33},{33,65},{65,97},{97,1},{2,34}... | collective-permute-start | bytes 589832 | tf_op jit(solution)/shard_map/ppermute | solution.py:34
  107.9 27.2 %collective-permute-start.8 = (f32[3,128,128]{2,1,0:T(8,128)S(1)}, f32[3,128,128]{2,1,0:T(8,128)S(1)}, u32[]{:S(2)}, u32[]{:S(2)}) collective-permute-start(f32[3,128,128]{2,1,0:T(8,128)S(1)} %get-tuple-element.15), channel_id=1, source_target_pairs={{0,96},{32,0},{64,32},{96,64},{1,97},{33,1},{65,33},{97,65},{2,98}... | collective-permute-start | bytes 589832 | tf_op jit(solution)/shard_map/ppermute | solution.py:34
  119.6 21.0 %collective-permute-start.5 = (f32[3,128,128]{2,1,0:T(8,128)S(1)}, f32[3,128,128]{2,1,0:T(8,128)S(1)}, u32[]{:S(2)}, u32[]{:S(2)}) collective-permute-start(f32[3,128,128]{2,1,0:T(8,128)S(1)} %collective-permute-done.3.refs_0_), channel_id=1, source_target_pairs={{0,32},{32,64},{64,96},{96,0},{1,33},{33,65},{65,97},{97,1},{2,34}... | collective-permute-start | bytes 589832 | tf_op jit(solution)/shard_map/ppermute | solution.py:34
  119.6 21.0 %collective-permute-start.7 = (f32[3,128,128]{2,1,0:T(8,128)S(1)}, f32[3,128,128]{2,1,0:T(8,128)S(1)}, u32[]{:S(2)}, u32[]{:S(2)}) collective-permute-start(f32[3,128,128]{2,1,0:T(8,128)S(1)} %collective-permute-done.6.refs_5_), channel_id=1, source_target_pairs={{0,96},{32,0},{64,32},{96,64},{1,97},{33,1},{65,33},{97,65},{2,98}... | collective-permute-start | bytes 589832 | tf_op jit(solution)/shard_map/ppermute | solution.py:34
  130.5 34.5 %collective-permute-start = (f32[2,128,128]{2,1,0:T(8,128)S(1)}, f32[2,128,128]{2,1,0:T(8,128)S(1)}, u32[]{:S(2)}, u32[]{:S(2)}) collective-permute-start(f32[2,128,128]{2,1,0:T(8,128)S(1)} %covariance.2), channel_id=1, source_target_pairs={{0,32},{32,64},{64,96},{96,0},{1,33},{33,65},{65,97},{97,1},{2,34}... | collective-permute-start | bytes 393224 | tf_op jit(solution)/shard_map/ppermute | solution.py:34
  132.2 32.9 %collective-permute-start.1 = (f32[2,128,128]{2,1,0:T(8,128)S(1)}, f32[2,128,128]{2,1,0:T(8,128)S(1)}, u32[]{:S(2)}, u32[]{:S(2)}) collective-permute-start(f32[2,128,128]{2,1,0:T(8,128)S(1)} %covariance.2), channel_id=1, source_target_pairs={{0,64},{32,96},{64,0},{96,32},{1,65},{33,97},{65,1},{97,33},{2,66}... | collective-permute-start | bytes 393224 | tf_op jit(solution)/shard_map/ppermute | solution.py:34
  135.1 30.0 %collective-permute-start.2 = (f32[2,128,128]{2,1,0:T(8,128)S(1)}, f32[2,128,128]{2,1,0:T(8,128)S(1)}, u32[]{:S(2)}, u32[]{:S(2)}) collective-permute-start(f32[2,128,128]{2,1,0:T(8,128)S(1)} %covariance.2), channel_id=1, source_target_pairs={{0,96},{32,0},{64,32},{96,64},{1,97},{33,1},{65,33},{97,65},{2,98}... | collective-permute-start | bytes 393224 | tf_op jit(solution)/shard_map/ppermute | solution.py:34
  148.5 0.9 copy-start
  155.3 8.1 %copy-start.1 = (bf16[2,128,256]{2,1,0:T(8,128)(2,1)S(1)}, bf16[2,128,256]{2,1,0:T(8,128)(2,1)}, u32[]{:S(2)}) copy-start(bf16[2,128,256]{2,1,0:T(8,128)(2,1)} %copy.9) | copy-start | bytes 393220

commit v2 on v0

--- a/solution.py
+++ b/solution.py
@@ -14,8 +14,8 @@
 NTR_EASY = 3
 NS_STEPS = 12
 CBLK = 128
-CHUNKS = (5, 3)
-RESIDENT = 3
+CHUNKS = (6, 2)
+EARLY = 2
 
 decay_rate = 0.7
 diag_load = 0.1
@@ -320,38 +320,41 @@
     return table.astype(bf16).reshape(2 * block_len, 2 * block_len)
 
 
-def compress_kernel(table_ref, y_hbm, z_out, y_ref, in_sem, *held):
-    count, sources, per, _ = y_ref.shape
-    z_ref, out_sem = held if held else (z_out, None)
-    step = CBLK // per
-    half = CH
-
-    def load(i):
-        return pltpu.make_async_copy(y_hbm.at[:, i], y_ref.at[i], in_sem.at[i])
-
-    def save(i):
-        return pltpu.make_async_copy(z_ref.at[i], z_out.at[i], out_sem.at[i])
-
-    for i in range(count):
-        load(i).start()
-    for i in range(count):
-        load(i).wait()
-        for start in range(0, sources, step):
-            stop = min(start + 2 * step, sources)
-            y = y_ref[i, start:stop].reshape((stop - start) * per, 2 * half)
-            m = jnp.dot(table_ref[:, : y.shape[0]], y, preferred_element_type=f32)
-            r = pl.ds(start * per, CBLK)
-            z_ref[i, r, :half] = (m[:CBLK, :half] + m[CBLK:, half:]).astype(bf16)
-            z_ref[i, r, half:] = (m[:CBLK, half:] - m[CBLK:, :half]).astype(bf16)
+def make_compress_kernel(skip):
+    def compress_kernel(table_ref, y_hbm, z_out, y_ref, in_sem, *held):
+        count, sources, per, _ = y_ref.shape
+        z_ref, out_sem = held if held else (z_out, None)
+        step = CBLK // per
+        half = CH
+
+        def load(i):
+            return pltpu.make_async_copy(y_hbm.at[:, skip + i], y_ref.at[i], in_sem.at[i])
+
+        def save(i):
+            return pltpu.make_async_copy(z_ref.at[i], z_out.at[i], out_sem.at[i])
+
+        for i in range(count):
+            load(i).start()
+        for i in range(count):
+            load(i).wait()
+            for start in range(0, sources, step):
+                stop = min(start + 2 * step, sources)
+                y = y_ref[i, start:stop].reshape((stop - start) * per, 2 * half)
+                m = jnp.dot(table_ref[:, : y.shape[0]], y, preferred_element_type=f32)
+                r = pl.ds(start * per, CBLK)
+                z_ref[i, r, :half] = (m[:CBLK, :half] + m[CBLK:, half:]).astype(bf16)
+                z_ref[i, r, half:] = (m[:CBLK, half:] - m[CBLK:, :half]).astype(bf16)
+            if held:
+                save(i).start()
         if held:
-            save(i).start()
-    if held:
-        for i in range(count):
-            save(i).wait()
-
-
-def compress(owned, table):
-    sources, count, per, width = owned.shape
+            for i in range(count):
+                save(i).wait()
+
+    return compress_kernel
+
+
+def compress(owned, table, skip, count, stay):
+    sources, _, per, width = owned.shape
     vmem = pl.BlockSpec(memory_space=pltpu.VMEM)
     anywhere = pl.BlockSpec(memory_space=pl.ANY)
     shape = (count, sources * per, width)
@@ -359,34 +362,35 @@
         pltpu.VMEM((count, sources, per, width), bf16),
         pltpu.SemaphoreType.DMA((count,)),
     ]
-    if count > RESIDENT:
+    if not stay:
         scratch += [pltpu.VMEM(shape, bf16), pltpu.SemaphoreType.DMA((count,))]
     return pl.pallas_call(
-        compress_kernel,
-        out_shape=pltpu.HBM(shape, bf16) if count > RESIDENT else jax.ShapeDtypeStruct(shape, bf16),
+        make_compress_kernel(skip),
+        out_shape=jax.ShapeDtypeStruct(shape, bf16) if stay else pltpu.HBM(shape, bf16),
         in_specs=[vmem, anywhere],
-        out_specs=anywhere if count > RESIDENT else vmem,
+        out_specs=vmem if stay else anywhere,
         scratch_shapes=scratch,
         compiler_params=params(32),
         name="compress",
     )(table, owned)
 
 
-def make_beams_kernel(first, aliased):
-    def beams_kernel(w_ref, z_in, *refs):
-        o_hbm, o_ref, out_sem, *held = refs[aliased:]
-        z_ref, in_sem = held if held else (z_in, None)
-        count, rows, _ = z_ref.shape
+def make_beams_kernel(first, skip, parts, aliased):
+    def beams_kernel(w_ref, *refs):
+        z_in = entries(refs[:parts])
+        o_hbm, o_ref, out_sem, *held = refs[parts + aliased :]
+        count, rows, _ = o_ref.shape
         pieces = out_sem.shape[1]
         step = rows // pieces
 
         def load(i):
-            return pltpu.make_async_copy(z_in.at[i], z_ref.at[i], in_sem.at[i])
+            ref, j = z_in[skip + i]
+            return pltpu.make_async_copy(ref.at[j], held[0].at[i], held[1].at[i])
 
         def save(i, p):
-            piece = pl.ds(p * step, step)
+            r = pl.ds(p * step, step)
             return pltpu.make_async_copy(
-                o_ref.at[i, piece], o_hbm.at[first + i, piece], out_sem.at[i, p]
+                o_ref.at[i, r], o_hbm.at[first + skip + i, r], out_sem.at[i, p]
             )
 
         if held:
@@ -395,10 +399,14 @@
         for i in range(count):
             if held:
                 load(i).wait()
+                source = held[0].at[i]
+            else:
+                ref, j = z_in[skip + i]
+                source = ref.at[j]
             for p in range(pieces):
                 r = pl.ds(p * step, step)
                 o_ref[i, r] = jnp.dot(
-                    z_ref[i, r], w_ref[i], preferred_element_type=f32
+                    source[r], w_ref[skip + i], preferred_element_type=f32
                 ).astype(bf16)
                 save(i, p).start()
         for i in range(count):
@@ -408,36 +416,29 @@
     return beams_kernel
 
 
-def form_beams(z, weights, held, bins, first):
-    count, rows, _ = z.shape
+def form_beams(z, weights, held, bins, first, skip, count, stay):
+    rows = z[0].shape[1]
     width = weights.shape[2]
-    resident = count <= RESIDENT
     vmem = pl.BlockSpec(memory_space=pltpu.VMEM)
     anywhere = pl.BlockSpec(memory_space=pl.ANY)
-    in_specs = [vmem, vmem if resident else anywhere]
-    operands = [weights, z]
-    aliases = {}
-    if held is not None:
-        in_specs.append(anywhere)
-        operands.append(held)
-        aliases = {2: 0}
-    pieces = 2 if resident else 1
+    before = [] if held is None else [held]
+    pieces = 2 if stay else 1
     scratch = [
         pltpu.VMEM((count, rows, width), bf16),
         pltpu.SemaphoreType.DMA((count, pieces)),
     ]
-    if not resident:
-        scratch += [pltpu.VMEM(z.shape, bf16), pltpu.SemaphoreType.DMA((count,))]
+    if not stay:
+        scratch += [pltpu.VMEM((count, rows, width), bf16), pltpu.SemaphoreType.DMA((count,))]
     return pl.pallas_call(
-        make_beams_kernel(first, len(aliases)),
+        make_beams_kernel(first, skip, len(z), len(before)),
         out_shape=jax.ShapeDtypeStruct((bins, rows, width), bf16),
-        in_specs=in_specs,
+        in_specs=[vmem] + [vmem if stay else anywhere] * len(z) + [anywhere] * len(before),
         out_specs=anywhere,
         scratch_shapes=scratch,
-        input_output_aliases=aliases,
-        compiler_params=params(32 if resident else 59),
+        input_output_aliases={1 + len(z): 0} if before else {},
+        compiler_params=params(32 if stay else 60),
         name="beams",
-    )(*operands)
+    )(weights, *z, *before)
 
 
 def chain(echoes, train_blocks, hard_bins, owner_map, code_phase):
@@ -458,13 +459,18 @@
             sent, owned[-1] = lax.optimization_barrier((sent, owned[-1]))
         owned.append(lax.all_to_all(sent, "blk", split_axis=0, concat_axis=0, tiled=True))
     result = None
-    for first, y in zip(firsts, owned):
+    for g, (first, y) in enumerate(zip(firsts, owned)):
         count = y.shape[1]
-        pieces = [count // 2, count - count // 2] if count > 2 else [count]
+        last = g == len(CHUNKS) - 1
+        pieces = [count] if last else [count // 2, count - count // 2]
         parts = earlier(covariance(y, blocks, hard, first, pieces))
-        z = compress(y, table)
+        z = []
+        for n, some in enumerate(pieces):
+            z.append(compress(y, table, sum(pieces[:n]), some, last))
         weights = beam_weights(parts)
-        result = form_beams(z, weights, result, bins, first)
+        spans = [(0, count)] if last else [(0, EARLY), (EARLY, count - EARLY)]
+        for skip, some in spans:
+            result = form_beams(z, weights, result, bins, first, skip, some, last)
     return result[None]
 
 

time: 177 us -> 178 us (level)
  Pallas kernels: 49.5 us -> 56.2 us
  waiting for transfers between devices: 92.8 us -> 86.4 us
  starting transfers between devices: 29.8 us -> 27.9 us
    all_to_all x2, waiting for transfers between devices: 90.1 us -> 77.3 us  [chain(): lax.all_to_all(sent, 'blk', split_axis=0, concat_axis=0, tiled=True)]
    ppermute x12 -> x9, waiting for transfers between devices: 2.73 us -> 9.04 us  [shifted(): lax.ppermute(x, 'segment', [(i, (i + by) % peers) for i in range(peers)])]
    pallas_call x4 -> x6, Pallas kernels: 17 us -> 23.2 us  [the longest x3 12.7 us: form_beams(): pl.pallas_call(make_beams_kernel(first, skip, len(z), len(before)), out_s...]
    ppermute x12 -> x9, starting transfers between devices: 17.3 us -> 15.5 us  [shifted(): lax.ppermute(x, 'segment', [(i, (i + by) % peers) for i in range(peers)])]
  transfers between devices with their start and end apart: 14 -> 11, of which waited for: 4 -> 3; matrix products, arithmetic and copies ran while one was open for 2% -> 3% of each run, Pallas kernels for 20% -> 23%
where the time goes in v2:
time: 178 us; the launch traced here: 177 us
  waiting for transfers between devices  86.4 us (49%)
  Pallas kernels  56.2 us (32%)
  starting transfers between devices  27.9 us (16%)
  matrix products  3.55 us (2%)
  local copies, waits for them, and re-layouts  2.37 us (1%)
    all_to_all x2, waiting for transfers between devices, chain(): lax.all_to_all(sent, 'blk', split_axis=0, concat_axis=0, tiled=True)  77.3 us
    ppermute x9, starting transfers between devices, shifted(): lax.ppermute(x, 'segment', [(i, (i + by) % peers) for i in range(peers)])  15.5 us
    pallas_call x2, Pallas kernels, doppler(): pl.pallas_call(make_doppler_kernel(owners, first, count), out_shape=pltpu...  15.5 us
    pallas_call x2, Pallas kernels, beam_weights(): pl.pallas_call(weights_kernel, out_shape=jax.ShapeDtypeStruct((count, 2 *...  13 us
    pallas_call x3, Pallas kernels, form_beams(): pl.pallas_call(make_beams_kernel(first, skip, len(z), len(before)), out_s...  12.7 us
    all_to_all x2, starting transfers between devices, chain(): lax.all_to_all(sent, 'blk', split_axis=0, concat_axis=0, tiled=True)  12.4 us
    pallas_call x3, Pallas kernels, compress(): pl.pallas_call(make_compress_kernel(skip), out_shape=jax.ShapeDtypeStruct...  10.5 us
    ppermute x9, waiting for transfers between devices, shifted(): lax.ppermute(x, 'segment', [(i, (i + by) % peers) for i in range(peers)])  9.04 us
  transfers between devices with their start and end apart: 11, of which 3 were waited for; matrix products, arithmetic and copies ran while one was open for 3% of the time, Pallas kernels for 23%

profile of v2, /device:TPU:0, one launch (start us, length us, event | category | flops | bytes accessed | tf_op | source)
XLA Modules:
  0.0 177.4 jit_solution(954030369706363793)
XLA Ops:
  0.0 8.7 %doppler.3 = bf16[192,64,256]{2,1,0:T(8,128)(2,1)} custom-call(s32[1,256]{1,0:T(1,128)} %bitcast.26, bf16[64,128,512]{2,1,0:T(8,128)(2,1)} %bitcast.22), custom_call_target="tpu_custom_call" | custom-call | tf_op jit(solution)/shard_map/doppler/pallas_call | solution.py:123
  8.7 8.4 %all-to-all-start = ((bf16[32,6,64,256]{3,2,1,0:T(8,128)(2,1)}), bf16[32,6,64,256]{3,2,1,0:T(8,128)(2,1)}, u32[]{:S(2)}, u32[]{:S(2)}) async-start(bf16[32,6,64,256]{3,2,1,0:T(8,128)(2,1)} %bitcast.24), calls=%async_computation | async-start | bytes 12582912 | tf_op jit(solution)/shard_map/all_to_all | solution.py:460
  17.1 6.8 %doppler.2 = bf16[64,64,256]{2,1,0:T(8,128)(2,1)} custom-call(s32[1,256]{1,0:T(1,128)} %bitcast.27, bf16[64,128,512]{2,1,0:T(8,128)(2,1)} %bitcast.23), custom_call_target="tpu_custom_call" | custom-call | tf_op jit(solution)/shard_map/doppler/pallas_call | solution.py:123
  23.9 0.0 copy-start.3
  23.9 0.0 copy-start.2
  23.9 71.1 %all-to-all-done.y_ref.y_hbm = bf16[32,6,64,256]{3,2,1,0:T(8,128)(2,1)} async-done(((bf16[32,6,64,256]{3,2,1,0:T(8,128)(2,1)}), bf16[32,6,64,256]{3,2,1,0:T(8,128)(2,1)}, u32[]{:S(2)}, u32[]{:S(2)}) %all-to-all-start) | async-done | bytes 6291488 | tf_op jit(solution)/shard_map/all_to_all | solution.py:460
  95.0 4.0 %all-to-all-start.1 = ((bf16[32,2,64,256]{3,2,1,0:T(8,128)(2,1)}), bf16[32,2,64,256]{3,2,1,0:T(8,128)(2,1)S(1)}, u32[]{:S(2)}, u32[]{:S(2)}) async-start(bf16[32,2,64,256]{3,2,1,0:T(8,128)(2,1)} %bitcast.25), calls=%async_computation.1 | async-start | bytes 4194304 | tf_op jit(solution)/shard_map/all_to_all | solution.py:460
  99.0 0.8 copy.8
  99.8 0.7 iota_subtract_fusion
  100.4 0.7 copy-done.1
  101.1 3.1 %covariance.3 = (f32[3,128,128]{2,1,0:T(8,128)S(1)}, f32[3,128,128]{2,1,0:T(8,128)}) custom-call(s32[8,6]{1,0:T(8,128)S(1)} %bitcast.18, s32[8]{0:T(128)S(1)} %bitcast.20, bf16[32,6,64,256]{3,2,1,0:T(8,128)(2,1)} %all-to-all-done.y_ref.y_hbm), custom_call_target="tpu_custom_call" | custom-call | tf_op jit(solution)/shard_map/covariance/pallas_call | solution.py:193
  104.2 3.1 %collective-permute-start.6 = (f32[3,128,128]{2,1,0:T(8,128)}, f32[3,128,128]{2,1,0:T(8,128)S(1)}, u32[]{:S(2)}, u32[]{:S(2)}) collective-permute-start(f32[3,128,128]{2,1,0:T(8,128)} %get-tuple-element.16), channel_id=1, source_target_pairs={{0,96},{32,0},{64,32},{96,64},{1,97},{33,1},{65,33},{97,65},{2,98}... | collective-permute-start | bytes 589832 | tf_op jit(solution)/shard_map/ppermute | solution.py:34
  107.3 0.0 collective-permute-start.4
  107.3 0.6 collective-permute-start.3
  107.9 2.7 %collective-permute-start.8 = (f32[3,128,128]{2,1,0:T(8,128)S(1)}, f32[3,128,128]{2,1,0:T(8,128)S(1)}, u32[]{:S(2)}, u32[]{:S(2)}) collective-permute-start(f32[3,128,128]{2,1,0:T(8,128)S(1)} %get-tuple-element.15), channel_id=1, source_target_pairs={{0,96},{32,0},{64,32},{96,64},{1,97},{33,1},{65,33},{97,65},{2,98}... | collective-permute-start | bytes 589832 | tf_op jit(solution)/shard_map/ppermute | solution.py:34
  110.6 9.0 %collective-permute-done.3.refs_0_ = f32[3,128,128]{2,1,0:T(8,128)S(1)} collective-permute-done((f32[3,128,128]{2,1,0:T(8,128)S(1)}, f32[3,128,128]{2,1,0:T(8,128)S(1)}, u32[]{:S(2)}, u32[]{:S(2)}) %collective-permute-start.3) | collective-permute-done | bytes 196640 | tf_op jit(solution)/shard_map/ppermute | solution.py:34
  119.6 3.2 %collective-permute-start.7 = (f32[3,128,128]{2,1,0:T(8,128)S(1)}, f32[3,128,128]{2,1,0:T(8,128)S(1)}, u32[]{:S(2)}, u32[]{:S(2)}) collective-permute-start(f32[3,128,128]{2,1,0:T(8,128)S(1)} %collective-permute-done.6.refs_5_), channel_id=1, source_target_pairs={{0,96},{32,0},{64,32},{96,64},{1,97},{33,1},{65,33},{97,65},{2,98}... | collective-permute-start | bytes 589832 | tf_op jit(solution)/shard_map/ppermute | solution.py:34
  122.9 6.2 %all-to-all-done.1.y_ref.y_hbm = bf16[32,2,64,256]{3,2,1,0:T(8,128)(2,1)S(1)} async-done(((bf16[32,2,64,256]{3,2,1,0:T(8,128)(2,1)}), bf16[32,2,64,256]{3,2,1,0:T(8,128)(2,1)S(1)}, u32[]{:S(2)}, u32[]{:S(2)}) %all-to-all-start.1) | async-done | bytes 2097184 | tf_op jit(solution)/shard_map/all_to_all | solution.py:460
  129.1 1.4 covariance.2
  130.5 1.6 collective-permute-start
  132.2 2.9 %collective-permute-start.1 = (f32[2,128,128]{2,1,0:T(8,128)S(1)}, f32[2,128,128]{2,1,0:T(8,128)S(1)}, u32[]{:S(2)}, u32[]{:S(2)}) collective-permute-start(f32[2,128,128]{2,1,0:T(8,128)S(1)} %covariance.2), channel_id=1, source_target_pairs={{0,64},{32,96},{64,0},{96,32},{1,65},{33,97},{65,1},{97,33},{2,66}... | collective-permute-start | bytes 393224 | tf_op jit(solution)/shard_map/ppermute | solution.py:34
  135.1 1.3 collective-permute-start.2
  136.4 3.5 %fusion.2 = bf16[2,128,256]{2,0,1:T(2,128)(2,1)S(1)} fusion(s32[128,256]{1,0:T(8,128)} %iota_subtract_fusion, f32[1,64]{1,0:T(1,128)S(1)} %get-tuple-element.18, f32[1,64]{1,0:T(1,128)S(1)} %get-tuple-element.17), kind=kOutput, calls=%fused_computation.3 | convolution fusion | flops 52494592 | bytes 262656 | tf_op jit(solution)/shard_map/pql,kl->kpq/dot_general | solution.py:319
  140.0 4.4 %compress.5.refs_1_ = bf16[3,2048,256]{2,1,0:T(8,128)(2,1)} custom-call(bf16[256,256]{1,0:T(8,128)(2,1)S(1)} %bitcast.15, bf16[32,6,64,256]{3,2,1,0:T(8,128)(2,1)} %all-to-all-done.y_ref.y_hbm), custom_call_target="tpu_custom_call" | custom-call | tf_op jit(solution)/shard_map/compress/pallas_call | solution.py:367
  144.4 4.5 %compress.4.refs_0_ = bf16[3,2048,256]{2,1,0:T(8,128)(2,1)} custom-call(bf16[256,256]{1,0:T(8,128)(2,1)S(1)} %bitcast.16, bf16[32,6,64,256]{3,2,1,0:T(8,128)(2,1)} %all-to-all-done.y_ref.y_hbm), custom_call_target="tpu_custom_call" | custom-call | tf_op jit(solution)/shard_map/compress/pallas_call | solution.py:367
  148.9 8.1 %weights.3.w_ref = bf16[6,256,256]{2,1,0:T(8,128)(2,1)S(1)} custom-call(f32[3,128,128]{2,1,0:T(8,128)S(1)} %collective-permute-done.3.refs_0_, f32[3,128,128]{2,1,0:T(8,128)S(1)} %collective-permute-done.4.refs_1_, f32[3,128,128]{2,1,0:T(8,128)S(1)} %collective-permute-done.5.refs_2_, f32[3,128,128]{2,1,0:T(8,128)S(1)} %collective-permute-done.7.refs_3_, ...), custom_call_target="tpu_custom_call" | custom-call | tf_op jit(solution)/shard_map/weights/pallas_call | solution.py:289
  157.0 0.9 copy-done
  157.9 4.7 %beams.3.refs_2_ = bf16[8,2048,256]{2,1,0:T(8,128)(2,1)} custom-call(bf16[6,256,256]{2,1,0:T(8,128)(2,1)} %copy-done, bf16[3,2048,256]{2,1,0:T(8,128)(2,1)} %compress.4.refs_0_, bf16[3,2048,256]{2,1,0:T(8,128)(2,1)} %compress.5.refs_1_), custom_call_target="tpu_custom_call" | custom-call | tf_op jit(solution)/shard_map/beams/pallas_call | solution.py:432
  162.7 6.2 %beams.4.refs_1_ = bf16[8,2048,256]{2,1,0:T(8,128)(2,1)} custom-call(bf16[6,256,256]{2,1,0:T(8,128)(2,1)} %copy-done, bf16[3,2048,256]{2,1,0:T(8,128)(2,1)} %compress.4.refs_0_, bf16[3,2048,256]{2,1,0:T(8,128)(2,1)} %compress.5.refs_1_, bf16[8,2048,256]{2,1,0:T(8,128)(2,1)} %beams.3.refs_2_), custom_call_target="tpu_custom_call", output_to_operand_aliasing={{}: (3, {})} | custom-call | tf_op jit(solution)/shard_map/beams/pallas_call | solution.py:432
  168.8 1.6 compress.3.refs_0_
  170.5 5.0 %weights.2.w_ref = bf16[2,256,256]{2,1,0:T(8,128)(2,1)S(1)} custom-call(f32[2,128,128]{2,1,0:T(8,128)S(1)} %collective-permute-done.refs_0_, f32[2,128,128]{2,1,0:T(8,128)S(1)} %collective-permute-done.1.refs_1_, f32[2,128,128]{2,1,0:T(8,128)S(1)} %collective-permute-done.2.refs_2_), custom_call_target="tpu_custom_call" | custom-call | tf_op jit(solution)/shard_map/weights/pallas_call | solution.py:289
  175.4 1.8 %beams.5 = bf16[8,2048,256]{2,1,0:T(8,128)(2,1)} custom-call(bf16[2,256,256]{2,1,0:T(8,128)(2,1)S(1)} %weights.2.w_ref, bf16[2,2048,256]{2,1,0:T(8,128)(2,1)S(1)} %compress.3.refs_0_, bf16[8,2048,256]{2,1,0:T(8,128)(2,1)} %beams.4.refs_1_), custom_call_target="tpu_custom_call", output_to_operand_aliasing={{}: (2, {})} | custom-call | tf_op jit(solution)/shard_map/beams/pallas_call | solution.py:432
  (15 shorter events, 0.1 us)
Async XLA Ops:
  8.7 86.3 %all-to-all-start = ((bf16[32,6,64,256]{3,2,1,0:T(8,128)(2,1)}), bf16[32,6,64,256]{3,2,1,0:T(8,128)(2,1)}, u32[]{:S(2)}, u32[]{:S(2)}) async-start(bf16[32,6,64,256]{3,2,1,0:T(8,128)(2,1)} %bitcast.24), calls=%async_computation | async-start | bytes 12582912 | tf_op jit(solution)/shard_map/all_to_all | solution.py:460
  23.9 86.7 %copy-start.3 = (f32[64]{0:T(128)S(1)}, f32[64]{0:T(128)}, u32[]{:S(2)}) copy-start(f32[64]{0:T(128)} %param.9) | copy-start | bytes 772
  23.9 105.2 %copy-start.2 = (s32[1,8]{1,0:T(1,128)S(1)}, s32[1,8]{1,0:T(1,128)}, u32[]{:S(2)}) copy-start(s32[1,8]{1,0:T(1,128)} %param.7) | copy-start | bytes 100
  95.0 34.1 %all-to-all-start.1 = ((bf16[32,2,64,256]{3,2,1,0:T(8,128)(2,1)}), bf16[32,2,64,256]{3,2,1,0:T(8,128)(2,1)S(1)}, u32[]{:S(2)}, u32[]{:S(2)}) async-start(bf16[32,2,64,256]{3,2,1,0:T(8,128)(2,1)} %bitcast.25), calls=%async_computation.1 | async-start | bytes 4194304 | tf_op jit(solution)/shard_map/all_to_all | solution.py:460
  100.4 0.7 copy-start.1
  104.2 15.4 %collective-permute-start.6 = (f32[3,128,128]{2,1,0:T(8,128)}, f32[3,128,128]{2,1,0:T(8,128)S(1)}, u32[]{:S(2)}, u32[]{:S(2)}) collective-permute-start(f32[3,128,128]{2,1,0:T(8,128)} %get-tuple-element.16), channel_id=1, source_target_pairs={{0,96},{32,0},{64,32},{96,64},{1,97},{33,1},{65,33},{97,65},{2,98}... | collective-permute-start | bytes 589832 | tf_op jit(solution)/shard_map/ppermute | solution.py:34
  107.3 24.9 %collective-permute-start.4 = (f32[3,128,128]{2,1,0:T(8,128)}, f32[3,128,128]{2,1,0:T(8,128)S(1)}, u32[]{:S(2)}, u32[]{:S(2)}) collective-permute-start(f32[3,128,128]{2,1,0:T(8,128)} %get-tuple-element.16), channel_id=1, source_target_pairs={{0,32},{32,64},{64,96},{96,0},{1,33},{33,65},{65,97},{97,1},{2,34}... | collective-permute-start | bytes 589832 | tf_op jit(solution)/shard_map/ppermute | solution.py:34
  107.3 12.3 %collective-permute-start.3 = (f32[3,128,128]{2,1,0:T(8,128)S(1)}, f32[3,128,128]{2,1,0:T(8,128)S(1)}, u32[]{:S(2)}, u32[]{:S(2)}) collective-permute-start(f32[3,128,128]{2,1,0:T(8,128)S(1)} %get-tuple-element.15), channel_id=1, source_target_pairs={{0,32},{32,64},{64,96},{96,0},{1,33},{33,65},{65,97},{97,1},{2,34}... | collective-permute-start | bytes 589832 | tf_op jit(solution)/shard_map/ppermute | solution.py:34
  107.9 27.2 %collective-permute-start.8 = (f32[3,128,128]{2,1,0:T(8,128)S(1)}, f32[3,128,128]{2,1,0:T(8,128)S(1)}, u32[]{:S(2)}, u32[]{:S(2)}) collective-permute-start(f32[3,128,128]{2,1,0:T(8,128)S(1)} %get-tuple-element.15), channel_id=1, source_target_pairs={{0,96},{32,0},{64,32},{96,64},{1,97},{33,1},{65,33},{97,65},{2,98}... | collective-permute-start | bytes 589832 | tf_op jit(solution)/shard_map/ppermute | solution.py:34
  119.6 29.3 %collective-permute-start.5 = (f32[3,128,128]{2,1,0:T(8,128)S(1)}, f32[3,128,128]{2,1,0:T(8,128)S(1)}, u32[]{:S(2)}, u32[]{:S(2)}) collective-permute-start(f32[3,128,128]{2,1,0:T(8,128)S(1)} %collective-permute-done.3.refs_0_), channel_id=1, source_target_pairs={{0,32},{32,64},{64,96},{96,0},{1,33},{33,65},{65,97},{97,1},{2,34}... | collective-permute-start | bytes 589832 | tf_op jit(solution)/shard_map/ppermute | solution.py:34
  119.6 29.3 %collective-permute-start.7 = (f32[3,128,128]{2,1,0:T(8,128)S(1)}, f32[3,128,128]{2,1,0:T(8,128)S(1)}, u32[]{:S(2)}, u32[]{:S(2)}) collective-permute-start(f32[3,128,128]{2,1,0:T(8,128)S(1)} %collective-permute-done.6.refs_5_), channel_id=1, source_target_pairs={{0,96},{32,0},{64,32},{96,64},{1,97},{33,1},{65,33},{97,65},{2,98}... | collective-permute-start | bytes 589832 | tf_op jit(solution)/shard_map/ppermute | solution.py:34
  130.5 39.9 %collective-permute-start = (f32[2,128,128]{2,1,0:T(8,128)S(1)}, f32[2,128,128]{2,1,0:T(8,128)S(1)}, u32[]{:S(2)}, u32[]{:S(2)}) collective-permute-start(f32[2,128,128]{2,1,0:T(8,128)S(1)} %covariance.2), channel_id=1, source_target_pairs={{0,32},{32,64},{64,96},{96,0},{1,33},{33,65},{65,97},{97,1},{2,34}... | collective-permute-start | bytes 393224 | tf_op jit(solution)/shard_map/ppermute | solution.py:34
  132.2 38.3 %collective-permute-start.1 = (f32[2,128,128]{2,1,0:T(8,128)S(1)}, f32[2,128,128]{2,1,0:T(8,128)S(1)}, u32[]{:S(2)}, u32[]{:S(2)}) collective-permute-start(f32[2,128,128]{2,1,0:T(8,128)S(1)} %covariance.2), channel_id=1, source_target_pairs={{0,64},{32,96},{64,0},{96,32},{1,65},{33,97},{65,1},{97,33},{2,66}... | collective-permute-start | bytes 393224 | tf_op jit(solution)/shard_map/ppermute | solution.py:34
  135.1 35.4 %collective-permute-start.2 = (f32[2,128,128]{2,1,0:T(8,128)S(1)}, f32[2,128,128]{2,1,0:T(8,128)S(1)}, u32[]{:S(2)}, u32[]{:S(2)}) collective-permute-start(f32[2,128,128]{2,1,0:T(8,128)S(1)} %covariance.2), channel_id=1, source_target_pairs={{0,96},{32,0},{64,32},{96,64},{1,97},{33,1},{65,33},{97,65},{2,98}... | collective-permute-start | bytes 393224 | tf_op jit(solution)/shard_map/ppermute | solution.py:34
  157.0 0.9 copy-start

commit v3 on v0

--- a/solution.py
+++ b/solution.py
@@ -14,8 +14,8 @@
 NTR_EASY = 3
 NS_STEPS = 12
 CBLK = 128
-CHUNKS = (5, 3)
-RESIDENT = 3
+CHUNKS = (6, 2)
+RESIDENT = 6
 
 decay_rate = 0.7
 diag_load = 0.1
@@ -460,7 +460,7 @@
     result = None
     for first, y in zip(firsts, owned):
         count = y.shape[1]
-        pieces = [count // 2, count - count // 2] if count > 2 else [count]
+        pieces = [count // 2, count - count // 2] if count > 3 else [count]
         parts = earlier(covariance(y, blocks, hard, first, pieces))
         z = compress(y, table)
         weights = beam_weights(parts)

time: 177 us -> 165 us (0.932)
  the two profiles are of different devices: /device:TPU:0 before, /device:TPU:8 now
where the time goes in v3:
time: 165 us; the launch traced here: 164 us
  waiting for transfers between devices  90.1 us (55%)
  Pallas kernels  45 us (27%)
  starting transfers between devices  23.2 us (14%)
  matrix products  3.55 us (2%)
    all_to_all x2, waiting for transfers between devices, chain(): lax.all_to_all(sent, 'blk', split_axis=0, concat_axis=0, tiled=True)  83.3 us
    pallas_call x2, Pallas kernels, doppler(): pl.pallas_call(make_doppler_kernel(owners, first, count), out_shape=pltpu...  15.4 us
    pallas_call x2, Pallas kernels, beam_weights(): pl.pallas_call(weights_kernel, out_shape=jax.ShapeDtypeStruct((count, 2 *...  13 us
    all_to_all x2, starting transfers between devices, chain(): lax.all_to_all(sent, 'blk', split_axis=0, concat_axis=0, tiled=True)  12.3 us
    ppermute x9, starting transfers between devices, shifted(): lax.ppermute(x, 'segment', [(i, (i + by) % peers) for i in range(peers)])  10.9 us
    pallas_call x2, Pallas kernels, compress(): pl.pallas_call(compress_kernel, out_shape=pltpu.HBM(shape, bf16) if count...  7.17 us
    ppermute x9, waiting for transfers between devices, shifted(): lax.ppermute(x, 'segment', [(i, (i + by) % peers) for i in range(peers)])  6.76 us
    pallas_call x2, Pallas kernels, form_beams(): pl.pallas_call(make_beams_kernel(first, len(aliases)), out_shape=jax.Shap...  4.99 us
  transfers between devices with their start and end apart: 11, of which 4 were waited for; matrix products, arithmetic and copies ran while one was open for 3% of the time, Pallas kernels for 18%

profile of v3, /device:TPU:8, one launch (start us, length us, event | category | flops | bytes accessed | tf_op | source)
XLA Modules:
  0.0 164.4 jit_solution(14210046536327007801)
XLA Ops:
  0.0 8.7 %doppler.3 = bf16[192,64,256]{2,1,0:T(8,128)(2,1)} custom-call(s32[1,256]{1,0:T(1,128)} %bitcast.25, bf16[64,128,512]{2,1,0:T(8,128)(2,1)} %bitcast.21), custom_call_target="tpu_custom_call" | custom-call | tf_op jit(solution)/shard_map/doppler/pallas_call | solution.py:123
  8.7 8.3 %all-to-all-start = ((bf16[32,6,64,256]{3,2,1,0:T(8,128)(2,1)}), bf16[32,6,64,256]{3,2,1,0:T(8,128)(2,1)}, u32[]{:S(2)}, u32[]{:S(2)}) async-start(bf16[32,6,64,256]{3,2,1,0:T(8,128)(2,1)} %bitcast.23), calls=%async_computation | async-start | bytes 12582912 | tf_op jit(solution)/shard_map/all_to_all | solution.py:459
  17.0 6.7 %doppler.2 = bf16[64,64,256]{2,1,0:T(8,128)(2,1)} custom-call(s32[1,256]{1,0:T(1,128)} %bitcast.26, bf16[64,128,512]{2,1,0:T(8,128)(2,1)} %bitcast.22), custom_call_target="tpu_custom_call" | custom-call | tf_op jit(solution)/shard_map/doppler/pallas_call | solution.py:123
  23.7 0.0 copy-start.2
  23.7 0.0 copy-start.1
  23.7 71.1 %all-to-all-done.y_ref.y_hbm = bf16[32,6,64,256]{3,2,1,0:T(8,128)(2,1)} async-done(((bf16[32,6,64,256]{3,2,1,0:T(8,128)(2,1)}), bf16[32,6,64,256]{3,2,1,0:T(8,128)(2,1)}, u32[]{:S(2)}, u32[]{:S(2)}) %all-to-all-start) | async-done | bytes 6291488 | tf_op jit(solution)/shard_map/all_to_all | solution.py:459
  94.9 4.0 %all-to-all-start.1 = ((bf16[32,2,64,256]{3,2,1,0:T(8,128)(2,1)}), bf16[32,2,64,256]{3,2,1,0:T(8,128)(2,1)S(1)}, u32[]{:S(2)}, u32[]{:S(2)}) async-start(bf16[32,2,64,256]{3,2,1,0:T(8,128)(2,1)} %bitcast.24), calls=%async_computation.1 | async-start | bytes 4194304 | tf_op jit(solution)/shard_map/all_to_all | solution.py:459
  98.9 0.8 copy.7
  99.7 0.7 iota_subtract_fusion
  100.3 0.7 copy-done
  101.0 3.1 %covariance.3 = (f32[3,128,128]{2,1,0:T(8,128)}, f32[3,128,128]{2,1,0:T(8,128)S(1)}) custom-call(s32[8,6]{1,0:T(8,128)S(1)} %bitcast.17, s32[8]{0:T(128)S(1)} %bitcast.19, bf16[32,6,64,256]{3,2,1,0:T(8,128)(2,1)} %all-to-all-done.y_ref.y_hbm), custom_call_target="tpu_custom_call" | custom-call | tf_op jit(solution)/shard_map/covariance/pallas_call | solution.py:193
  104.0 0.5 collective-permute-start.8
  104.6 1.6 collective-permute-start.3
  106.1 1.4 collective-permute-start.6
  107.6 0.6 collective-permute-start.4
  108.2 5.4 %collective-permute-done.3.refs_0_ = f32[3,128,128]{2,1,0:T(8,128)S(1)} collective-permute-done((f32[3,128,128]{2,1,0:T(8,128)}, f32[3,128,128]{2,1,0:T(8,128)S(1)}, u32[]{:S(2)}, u32[]{:S(2)}) %collective-permute-start.3) | collective-permute-done | bytes 196640 | tf_op jit(solution)/shard_map/ppermute | solution.py:34
  113.6 0.6 collective-permute-start.5
  114.1 1.4 collective-permute-done.6.refs_5_
  115.5 1.3 collective-permute-start.7
  116.8 12.2 %all-to-all-done.1.y_ref.y_hbm = bf16[32,2,64,256]{3,2,1,0:T(8,128)(2,1)S(1)} async-done(((bf16[32,2,64,256]{3,2,1,0:T(8,128)(2,1)}), bf16[32,2,64,256]{3,2,1,0:T(8,128)(2,1)S(1)}, u32[]{:S(2)}, u32[]{:S(2)}) %all-to-all-start.1) | async-done | bytes 2097184 | tf_op jit(solution)/shard_map/all_to_all | solution.py:459
  129.0 1.4 covariance.2
  130.4 0.5 collective-permute-start.2
  130.9 2.6 %collective-permute-start.1 = (f32[2,128,128]{2,1,0:T(8,128)S(1)}, f32[2,128,128]{2,1,0:T(8,128)S(1)}, u32[]{:S(2)}, u32[]{:S(2)}) collective-permute-start(f32[2,128,128]{2,1,0:T(8,128)S(1)} %covariance.2), channel_id=1, source_target_pairs={{0,64},{32,96},{64,0},{96,32},{1,65},{33,97},{65,1},{97,33},{2,66}... | collective-permute-start | bytes 393224 | tf_op jit(solution)/shard_map/ppermute | solution.py:34
  133.5 0.0 collective-permute-done.4.refs_1_
  133.5 1.9 %collective-permute-start = (f32[2,128,128]{2,1,0:T(8,128)S(1)}, f32[2,128,128]{2,1,0:T(8,128)S(1)}, u32[]{:S(2)}, u32[]{:S(2)}) collective-permute-start(f32[2,128,128]{2,1,0:T(8,128)S(1)} %covariance.2), channel_id=1, source_target_pairs={{0,32},{32,64},{64,96},{96,0},{1,33},{33,65},{65,97},{97,1},{2,34}... | collective-permute-start | bytes 393224 | tf_op jit(solution)/shard_map/ppermute | solution.py:34
  135.4 3.5 %fusion.2 = bf16[2,128,256]{2,0,1:T(2,128)(2,1)S(1)} fusion(s32[128,256]{1,0:T(8,128)} %iota_subtract_fusion, f32[1,64]{1,0:T(1,128)S(1)} %get-tuple-element.18, f32[1,64]{1,0:T(1,128)S(1)} %get-tuple-element.17), kind=kOutput, calls=%fused_computation.3 | convolution fusion | flops 52494592 | bytes 262656 | tf_op jit(solution)/shard_map/pql,kl->kpq/dot_general | solution.py:319
  139.0 5.6 %compress.3.z_in = bf16[6,2048,256]{2,1,0:T(8,128)(2,1)S(1)} custom-call(bf16[256,256]{1,0:T(8,128)(2,1)S(1)} %bitcast.15, bf16[32,6,64,256]{3,2,1,0:T(8,128)(2,1)} %all-to-all-done.y_ref.y_hbm), custom_call_target="tpu_custom_call" | custom-call | tf_op jit(solution)/shard_map/compress/pallas_call | solution.py:364
  144.6 8.1 %weights.3.w_ref = bf16[6,256,256]{2,1,0:T(8,128)(2,1)S(1)} custom-call(f32[3,128,128]{2,1,0:T(8,128)S(1)} %collective-permute-done.3.refs_0_, f32[3,128,128]{2,1,0:T(8,128)S(1)} %collective-permute-done.4.refs_1_, f32[3,128,128]{2,1,0:T(8,128)S(1)} %collective-permute-done.5.refs_2_, f32[3,128,128]{2,1,0:T(8,128)S(1)} %collective-permute-done.7.refs_3_, ...), custom_call_target="tpu_custom_call" | custom-call | tf_op jit(solution)/shard_map/weights/pallas_call | solution.py:289
  152.7 3.2 %beams.2.refs_0_ = bf16[8,2048,256]{2,1,0:T(8,128)(2,1)} custom-call(bf16[6,256,256]{2,1,0:T(8,128)(2,1)S(1)} %weights.3.w_ref, bf16[6,2048,256]{2,1,0:T(8,128)(2,1)S(1)} %compress.3.z_in), custom_call_target="tpu_custom_call" | custom-call | tf_op jit(solution)/shard_map/beams/pallas_call | solution.py:431
  155.9 1.6 compress.2.z_in
  157.5 4.9 %weights.2.w_ref = bf16[2,256,256]{2,1,0:T(8,128)(2,1)S(1)} custom-call(f32[2,128,128]{2,1,0:T(8,128)S(1)} %collective-permute-done.refs_0_, f32[2,128,128]{2,1,0:T(8,128)S(1)} %collective-permute-done.1.refs_1_, f32[2,128,128]{2,1,0:T(8,128)S(1)} %collective-permute-done.2.refs_2_), custom_call_target="tpu_custom_call" | custom-call | tf_op jit(solution)/shard_map/weights/pallas_call | solution.py:289
  162.5 1.8 %beams.3 = bf16[8,2048,256]{2,1,0:T(8,128)(2,1)} custom-call(bf16[2,256,256]{2,1,0:T(8,128)(2,1)S(1)} %weights.2.w_ref, bf16[2,2048,256]{2,1,0:T(8,128)(2,1)S(1)} %compress.2.z_in, bf16[8,2048,256]{2,1,0:T(8,128)(2,1)} %beams.2.refs_0_), custom_call_target="tpu_custom_call", output_to_operand_aliasing={{}: (2, {})} | custom-call | tf_op jit(solution)/shard_map/beams/pallas_call | solution.py:431
  (11 shorter events, 0.1 us)
Async XLA Ops:
  8.7 86.2 %all-to-all-start = ((bf16[32,6,64,256]{3,2,1,0:T(8,128)(2,1)}), bf16[32,6,64,256]{3,2,1,0:T(8,128)(2,1)}, u32[]{:S(2)}, u32[]{:S(2)}) async-start(bf16[32,6,64,256]{3,2,1,0:T(8,128)(2,1)} %bitcast.23), calls=%async_computation | async-start | bytes 12582912 | tf_op jit(solution)/shard_map/all_to_all | solution.py:459
  23.7 84.5 %copy-start.2 = (f32[64]{0:T(128)S(1)}, f32[64]{0:T(128)}, u32[]{:S(2)}) copy-start(f32[64]{0:T(128)} %param.9) | copy-start | bytes 772
  23.7 105.3 %copy-start.1 = (s32[1,8]{1,0:T(1,128)S(1)}, s32[1,8]{1,0:T(1,128)}, u32[]{:S(2)}) copy-start(s32[1,8]{1,0:T(1,128)} %param.7) | copy-start | bytes 100
  94.9 34.1 %all-to-all-start.1 = ((bf16[32,2,64,256]{3,2,1,0:T(8,128)(2,1)}), bf16[32,2,64,256]{3,2,1,0:T(8,128)(2,1)S(1)}, u32[]{:S(2)}, u32[]{:S(2)}) async-start(bf16[32,2,64,256]{3,2,1,0:T(8,128)(2,1)} %bitcast.24), calls=%async_computation.1 | async-start | bytes 4194304 | tf_op jit(solution)/shard_map/all_to_all | solution.py:459
  100.3 0.7 copy-start
  104.0 26.9 %collective-permute-start.8 = (f32[3,128,128]{2,1,0:T(8,128)}, f32[3,128,128]{2,1,0:T(8,128)S(1)}, u32[]{:S(2)}, u32[]{:S(2)}) collective-permute-start(f32[3,128,128]{2,1,0:T(8,128)} %get-tuple-element.15), channel_id=1, source_target_pairs={{0,96},{32,0},{64,32},{96,64},{1,97},{33,1},{65,33},{97,65},{2,98}... | collective-permute-start | bytes 589832 | tf_op jit(solution)/shard_map/ppermute | solution.py:34
  104.6 9.0 %collective-permute-start.3 = (f32[3,128,128]{2,1,0:T(8,128)}, f32[3,128,128]{2,1,0:T(8,128)S(1)}, u32[]{:S(2)}, u32[]{:S(2)}) collective-permute-start(f32[3,128,128]{2,1,0:T(8,128)} %get-tuple-element.15), channel_id=1, source_target_pairs={{0,32},{32,64},{64,96},{96,0},{1,33},{33,65},{65,97},{97,1},{2,34}... | collective-permute-start | bytes 589832 | tf_op jit(solution)/shard_map/ppermute | solution.py:34
  106.1 9.4 %collective-permute-start.6 = (f32[3,128,128]{2,1,0:T(8,128)S(1)}, f32[3,128,128]{2,1,0:T(8,128)S(1)}, u32[]{:S(2)}, u32[]{:S(2)}) collective-permute-start(f32[3,128,128]{2,1,0:T(8,128)S(1)} %get-tuple-element.16), channel_id=1, source_target_pairs={{0,96},{32,0},{64,32},{96,64},{1,97},{33,1},{65,33},{97,65},{2,98}... | collective-permute-start | bytes 589832 | tf_op jit(solution)/shard_map/ppermute | solution.py:34
  107.6 25.9 %collective-permute-start.4 = (f32[3,128,128]{2,1,0:T(8,128)S(1)}, f32[3,128,128]{2,1,0:T(8,128)S(1)}, u32[]{:S(2)}, u32[]{:S(2)}) collective-permute-start(f32[3,128,128]{2,1,0:T(8,128)S(1)} %get-tuple-element.16), channel_id=1, source_target_pairs={{0,32},{32,64},{64,96},{96,0},{1,33},{33,65},{65,97},{97,1},{2,34}... | collective-permute-start | bytes 589832 | tf_op jit(solution)/shard_map/ppermute | solution.py:34
  113.6 31.0 %collective-permute-start.5 = (f32[3,128,128]{2,1,0:T(8,128)S(1)}, f32[3,128,128]{2,1,0:T(8,128)S(1)}, u32[]{:S(2)}, u32[]{:S(2)}) collective-permute-start(f32[3,128,128]{2,1,0:T(8,128)S(1)} %collective-permute-done.3.refs_0_), channel_id=1, source_target_pairs={{0,32},{32,64},{64,96},{96,0},{1,33},{33,65},{65,97},{97,1},{2,34}... | collective-permute-start | bytes 589832 | tf_op jit(solution)/shard_map/ppermute | solution.py:34
  115.5 29.1 %collective-permute-start.7 = (f32[3,128,128]{2,1,0:T(8,128)S(1)}, f32[3,128,128]{2,1,0:T(8,128)S(1)}, u32[]{:S(2)}, u32[]{:S(2)}) collective-permute-start(f32[3,128,128]{2,1,0:T(8,128)S(1)} %collective-permute-done.6.refs_5_), channel_id=1, source_target_pairs={{0,96},{32,0},{64,32},{96,64},{1,97},{33,1},{65,33},{97,65},{2,98}... | collective-permute-start | bytes 589832 | tf_op jit(solution)/shard_map/ppermute | solution.py:34
  130.4 27.1 %collective-permute-start.2 = (f32[2,128,128]{2,1,0:T(8,128)S(1)}, f32[2,128,128]{2,1,0:T(8,128)S(1)}, u32[]{:S(2)}, u32[]{:S(2)}) collective-permute-start(f32[2,128,128]{2,1,0:T(8,128)S(1)} %covariance.2), channel_id=1, source_target_pairs={{0,96},{32,0},{64,32},{96,64},{1,97},{33,1},{65,33},{97,65},{2,98}... | collective-permute-start | bytes 393224 | tf_op jit(solution)/shard_map/ppermute | solution.py:34
  130.9 26.6 %collective-permute-start.1 = (f32[2,128,128]{2,1,0:T(8,128)S(1)}, f32[2,128,128]{2,1,0:T(8,128)S(1)}, u32[]{:S(2)}, u32[]{:S(2)}) collective-permute-start(f32[2,128,128]{2,1,0:T(8,128)S(1)} %covariance.2), channel_id=1, source_target_pairs={{0,64},{32,96},{64,0},{96,32},{1,65},{33,97},{65,1},{97,33},{2,66}... | collective-permute-start | bytes 393224 | tf_op jit(solution)/shard_map/ppermute | solution.py:34
  133.5 24.0 %collective-permute-start = (f32[2,128,128]{2,1,0:T(8,128)S(1)}, f32[2,128,128]{2,1,0:T(8,128)S(1)}, u32[]{:S(2)}, u32[]{:S(2)}) collective-permute-start(f32[2,128,128]{2,1,0:T(8,128)S(1)} %covariance.2), channel_id=1, source_target_pairs={{0,32},{32,64},{64,96},{96,0},{1,33},{33,65},{65,97},{97,1},{2,34}... | collective-permute-start | bytes 393224 | tf_op jit(solution)/shard_map/ppermute | solution.py:34
